TPU v7x, 256 devices: a whole 4x4x8 slice. The times are simulated.
256 devices in a mesh: build: 16 (over x, y_hi, core), lat: 16 (over y_lo, z).
Axes of the slice: x: 4, y: 4 (y_hi: 2, y_lo: 2; y = y_hi * 2 + y_lo), z: 8, core: 2. Of those that a mesh axis runs over, the one named last changes fastest.
Arguments:
- density: float32 [32, 256, 1024], P('build', 'lat'), may hold values from 0.03 to 1
- support_mask: int32 [256, 1024], P('lat'), may hold values from 0 to 1
- pattern: int32 [27], replicated, may hold values from 0 to 7
- blocks: float32 [8, 3, 3], replicated, may hold values from -0.625 to 0.625
- displacement: float32 [3, 32, 256, 1024], P(None, 'build', 'lat'), may hold values from -6 to 6
- adjoint: float32 [3, 32, 256, 1024], P(None, 'build', 'lat'), may hold values from -6 to 6
Outputs:
- force: float32 [3, 32, 256, 1024], P(None, 'build', 'lat')
- sensitivity: float32 [32, 256, 1024], P('build', 'lat')
All inputs are finite; a program needn't handle non-finite values.
Results may differ from a plain program's by a relative error of at most 0.0003.
Values sent between devices are 32-bit elements; how exact they have to be, the bound alone decides.
No kernel may reach another device: no remote copies, remote signals or barrier semaphores. Data moves between devices by JAX's collectives and lax.ppermute only.
A program may use at most 64 MiB of HBM per device.

v0:
```python
import jax
import jax.numpy as jnp
from jax import lax
from jax.sharding import PartitionSpec as P

exponent = 16.0
smooth_eps = 0.0001
root_eps = 0.01
base_floor = 0.05
modulus_floor = 0.001
highest = lax.Precision.HIGHEST


def extended(shard, sides, width):
    for axis, dim in sides:
        devices, length = (lax.axis_size(axis), shard.shape[dim])
        up = [(i, (i + 1) % devices) for i in range(devices - 1)]
        down = [(j, i) for i, j in up]
        last = lax.slice_in_dim(shard, length - width, length, axis=dim)
        initial = lax.slice_in_dim(shard, 0, width, axis=dim)
        before = lax.ppermute(last, axis, up)
        after = lax.ppermute(initial, axis, down)
        shard = jnp.concatenate([before, shard, after], axis=dim)
    return shard


def from_behind(block, axis, distance):
    devices = range(lax.axis_size(axis))
    route = [(i - distance, i) for i in devices if i - distance in devices]
    return lax.ppermute(block, axis, route)


def cross_local(padded):
    centre = padded[1:-1]
    widened = jnp.pad(centre, ((0, 0), (1, 1)))
    return centre + padded[:-2] + padded[2:] + widened[:, :-2] + widened[:, 2:]


def forward_block(design, bottom, inside):

    def forward_layer(from_below, design_layer):
        padded = extended(from_below**exponent, (("lat", 0),), 1)
        support = cross_local(padded) ** (1.0 / exponent)
        differ = design_layer - support
        printed = (
            0.5
            * (design_layer + support - jnp.sqrt(differ * differ + smooth_eps) + root_eps)
            * inside
        )
        return (printed, (printed, support))

    _, (printed, support) = lax.scan(forward_layer, bottom, design)
    return (printed, support)


def backward_block(direct, printed, support, design, incoming, inside):
    safe_support = jnp.where(inside > 0.5, support, 1.0)

    def backward_layer(from_above, layer_items):
        direct_layer, printed_layer, support_layer, design_layer = layer_items
        padded = extended(from_above, (("lat", 0),), 1)
        weight_total = direct_layer + printed_layer ** (exponent - 1.0) * cross_local(padded)
        differ = design_layer - support_layer
        slope_term = differ / jnp.sqrt(differ * differ + smooth_eps)
        sensitivity = weight_total * 0.5 * (1.0 - slope_term)
        passed = (
            weight_total * 0.5 * (1.0 + slope_term) / support_layer ** (exponent - 1.0) * inside
        )
        return (passed, sensitivity)

    outgoing, sensitivity = lax.scan(
        backward_layer, incoming, (direct, printed, safe_support, design), reverse=True
    )
    return (sensitivity, outgoing)


def whole_forward(density, base_plane, position, build_count):
    inside = jnp.ones((density.shape[2],), jnp.float32)
    zero_block = jnp.zeros(density.shape, jnp.float32)

    def forward_section(section_number, carried):
        received = from_behind(carried[0][-1], "build", 1)
        bottom = jnp.where(position == 0, base_plane, received)
        return forward_block(density, bottom, inside)

    return lax.fori_loop(0, build_count, forward_section, (zero_block, zero_block))


def whole_backward(direct, printed, support, density, build_count):
    inside = jnp.ones((density.shape[2],), jnp.float32)
    zero_block = jnp.zeros(density.shape, jnp.float32)
    zero_plane = jnp.zeros(density.shape[1:], jnp.float32)

    def backward_section(section_number, carried):
        received = from_behind(carried[1], "build", -1)
        return backward_block(direct, printed, support, density, received, inside)

    sensitivity, _ = lax.fori_loop(0, build_count, backward_section, (zero_block, zero_plane))
    return sensitivity


def apply_blocks(rimmed, blocks_used, reverse):
    widened = jnp.pad(rimmed, ((0, 0), (0, 0), (0, 0), (1, 1)))
    layer_count = rimmed.shape[1] - 2
    width_x = rimmed.shape[2] - 2
    width_y = rimmed.shape[3]
    result = jnp.zeros((rimmed.shape[0], layer_count, width_x, width_y), jnp.float32)
    direction = -1 if reverse else 1
    number = 0
    for step_z in (-1, 0, 1):
        for step_x in (-1, 0, 1):
            for step_y in (-1, 0, 1):
                start_z = 1 + direction * step_z
                start_x = 1 + direction * step_x
                start_y = 1 + direction * step_y
                shifted = widened[
                    :,
                    start_z : start_z + layer_count,
                    start_x : start_x + width_x,
                    start_y : start_y + width_y,
                ]
                matrix = blocks_used[number].T if reverse else blocks_used[number]
                result = result + jnp.einsum("cd,dzxy->czxy", matrix, shifted, precision=highest)
                number += 1
    return result


def on_device(density, support_mask, pattern, blocks, displacement, adjoint):
    build_count = lax.axis_size("build")
    position = lax.axis_index("build")
    base_plane = base_floor + (1.0 - base_floor) * support_mask.astype(jnp.float32)
    printed, support = whole_forward(density, base_plane, position, build_count)
    modulus = modulus_floor + (1.0 - modulus_floor) * printed**3
    table_rows = blocks.shape[0]
    onehot = (pattern[:, None] == jnp.arange(table_rows, dtype=jnp.int32)[None, :]).astype(
        jnp.float32
    )
    blocks_used = jnp.dot(onehot, blocks.reshape(table_rows, 9), precision=highest).reshape(
        27, 3, 3
    )
    stacked = jnp.concatenate([modulus[None] * displacement, adjoint], 0)
    rimmed = extended(stacked, (("build", 1), ("lat", 2)), 1)
    loaded = rimmed[:3]
    pulled_in = rimmed[3:]
    force = apply_blocks(loaded, blocks_used, False)
    pulled = apply_blocks(pulled_in, blocks_used, True)
    direct = jnp.sum(displacement * pulled, axis=0) * (3.0 * (1.0 - modulus_floor)) * printed**2
    sensitivity = whole_backward(direct, printed, support, density, build_count)
    return (force, sensitivity)


def solution(mesh):
    in_specs = (
        P("build", "lat", None),
        P("lat", None),
        P(),
        P(),
        P(None, "build", "lat", None),
        P(None, "build", "lat", None),
    )
    out_specs = (P(None, "build", "lat", None), P("build", "lat", None))
    return jax.shard_map(
        on_device, mesh=mesh, in_specs=in_specs, out_specs=out_specs, check_vma=False
    )
```

profile of v0, /device:TPU:12, one launch (start us, length us, event | category | flops | bytes accessed | tf_op | source)
XLA Modules:
  0.0 1021.2 jit_solution(17448339726769081717)
XLA Ops:
  2.2 484.0 %while.77 = (s32[]{:T(128)}, f32[2,16,1024]{2,1,0:T(8,128)S(1)}, f32[2,16,1024]{2,1,0:T(8,128)}, pred[]{:T(512)}, f32[16,1024]{1,0:T(8,128)S(1)}, /*index=5*/f32...) while((s32[]{:T(128)}, f32[2,16,1024]{2,1,0:T(8,128)S(1)}, f32[2,16,1024]{2,1,0:T(8,128)}, pred[]{:T(512)}, ...), condition=%wide.region_3.4_spmd, body=%wide.region_0.3_spmd.sunk | while | flops 229380 | bytes 1761663 | solution.py:86
  10.3 27.0 %while.80 = (s32[]{:T(128)}, f32[16,1024]{1,0:T(8,128)S(1)}, f32[2,16,1024]{2,1,0:T(8,128)S(1)}, f32[2,16,1024]{2,1,0:T(8,128)S(1)}, f32[2,16,1024]{2,1,0:T(8,128)}, /*index=5*/s32[]{:T(128)}) while((s32[]{:T(128)}, f32[16,1024]{1,0:T(8,128)S(1)}, f32[2,16,1024]{2,1,0:T(8,128)S(1)}, f32[2,16,1024]{2,1,0:T(8,128)S(1)}, ...), condition=%wide.region_2.2_spmd, body=%wide.region_1.1_spmd.sunk | while | flops 212994 | bytes 647333 | solution.py:52
  45.9 21.2 %while.80 = (s32[]{:T(128)}, f32[16,1024]{1,0:T(8,128)S(1)}, f32[2,16,1024]{2,1,0:T(8,128)S(1)}, f32[2,16,1024]{2,1,0:T(8,128)S(1)}, f32[2,16,1024]{2,1,0:T(8,128)}, /*index=5*/s32[]{:T(128)}) while((s32[]{:T(128)}, f32[16,1024]{1,0:T(8,128)S(1)}, f32[2,16,1024]{2,1,0:T(8,128)S(1)}, f32[2,16,1024]{2,1,0:T(8,128)S(1)}, ...), condition=%wide.region_2.2_spmd, body=%wide.region_1.1_spmd.sunk | while | flops 212994 | bytes 647333 | solution.py:52
  75.8 21.2 %while.80 = (s32[]{:T(128)}, f32[16,1024]{1,0:T(8,128)S(1)}, f32[2,16,1024]{2,1,0:T(8,128)S(1)}, f32[2,16,1024]{2,1,0:T(8,128)S(1)}, f32[2,16,1024]{2,1,0:T(8,128)}, /*index=5*/s32[]{:T(128)}) while((s32[]{:T(128)}, f32[16,1024]{1,0:T(8,128)S(1)}, f32[2,16,1024]{2,1,0:T(8,128)S(1)}, f32[2,16,1024]{2,1,0:T(8,128)S(1)}, ...), condition=%wide.region_2.2_spmd, body=%wide.region_1.1_spmd.sunk | while | flops 212994 | bytes 647333 | solution.py:52
  105.7 21.2 %while.80 = (s32[]{:T(128)}, f32[16,1024]{1,0:T(8,128)S(1)}, f32[2,16,1024]{2,1,0:T(8,128)S(1)}, f32[2,16,1024]{2,1,0:T(8,128)S(1)}, f32[2,16,1024]{2,1,0:T(8,128)}, /*index=5*/s32[]{:T(128)}) while((s32[]{:T(128)}, f32[16,1024]{1,0:T(8,128)S(1)}, f32[2,16,1024]{2,1,0:T(8,128)S(1)}, f32[2,16,1024]{2,1,0:T(8,128)S(1)}, ...), condition=%wide.region_2.2_spmd, body=%wide.region_1.1_spmd.sunk | while | flops 212994 | bytes 647333 | solution.py:52
  135.6 21.2 %while.80 = (s32[]{:T(128)}, f32[16,1024]{1,0:T(8,128)S(1)}, f32[2,16,1024]{2,1,0:T(8,128)S(1)}, f32[2,16,1024]{2,1,0:T(8,128)S(1)}, f32[2,16,1024]{2,1,0:T(8,128)}, /*index=5*/s32[]{:T(128)}) while((s32[]{:T(128)}, f32[16,1024]{1,0:T(8,128)S(1)}, f32[2,16,1024]{2,1,0:T(8,128)S(1)}, f32[2,16,1024]{2,1,0:T(8,128)S(1)}, ...), condition=%wide.region_2.2_spmd, body=%wide.region_1.1_spmd.sunk | while | flops 212994 | bytes 647333 | solution.py:52
  165.5 21.2 %while.80 = (s32[]{:T(128)}, f32[16,1024]{1,0:T(8,128)S(1)}, f32[2,16,1024]{2,1,0:T(8,128)S(1)}, f32[2,16,1024]{2,1,0:T(8,128)S(1)}, f32[2,16,1024]{2,1,0:T(8,128)}, /*index=5*/s32[]{:T(128)}) while((s32[]{:T(128)}, f32[16,1024]{1,0:T(8,128)S(1)}, f32[2,16,1024]{2,1,0:T(8,128)S(1)}, f32[2,16,1024]{2,1,0:T(8,128)S(1)}, ...), condition=%wide.region_2.2_spmd, body=%wide.region_1.1_spmd.sunk | while | flops 212994 | bytes 647333 | solution.py:52
  195.3 21.2 %while.80 = (s32[]{:T(128)}, f32[16,1024]{1,0:T(8,128)S(1)}, f32[2,16,1024]{2,1,0:T(8,128)S(1)}, f32[2,16,1024]{2,1,0:T(8,128)S(1)}, f32[2,16,1024]{2,1,0:T(8,128)}, /*index=5*/s32[]{:T(128)}) while((s32[]{:T(128)}, f32[16,1024]{1,0:T(8,128)S(1)}, f32[2,16,1024]{2,1,0:T(8,128)S(1)}, f32[2,16,1024]{2,1,0:T(8,128)S(1)}, ...), condition=%wide.region_2.2_spmd, body=%wide.region_1.1_spmd.sunk | while | flops 212994 | bytes 647333 | solution.py:52
  225.2 21.2 %while.80 = (s32[]{:T(128)}, f32[16,1024]{1,0:T(8,128)S(1)}, f32[2,16,1024]{2,1,0:T(8,128)S(1)}, f32[2,16,1024]{2,1,0:T(8,128)S(1)}, f32[2,16,1024]{2,1,0:T(8,128)}, /*index=5*/s32[]{:T(128)}) while((s32[]{:T(128)}, f32[16,1024]{1,0:T(8,128)S(1)}, f32[2,16,1024]{2,1,0:T(8,128)S(1)}, f32[2,16,1024]{2,1,0:T(8,128)S(1)}, ...), condition=%wide.region_2.2_spmd, body=%wide.region_1.1_spmd.sunk | while | flops 212994 | bytes 647333 | solution.py:52
  255.1 21.2 %while.80 = (s32[]{:T(128)}, f32[16,1024]{1,0:T(8,128)S(1)}, f32[2,16,1024]{2,1,0:T(8,128)S(1)}, f32[2,16,1024]{2,1,0:T(8,128)S(1)}, f32[2,16,1024]{2,1,0:T(8,128)}, /*index=5*/s32[]{:T(128)}) while((s32[]{:T(128)}, f32[16,1024]{1,0:T(8,128)S(1)}, f32[2,16,1024]{2,1,0:T(8,128)S(1)}, f32[2,16,1024]{2,1,0:T(8,128)S(1)}, ...), condition=%wide.region_2.2_spmd, body=%wide.region_1.1_spmd.sunk | while | flops 212994 | bytes 647333 | solution.py:52
  285.0 21.2 %while.80 = (s32[]{:T(128)}, f32[16,1024]{1,0:T(8,128)S(1)}, f32[2,16,1024]{2,1,0:T(8,128)S(1)}, f32[2,16,1024]{2,1,0:T(8,128)S(1)}, f32[2,16,1024]{2,1,0:T(8,128)}, /*index=5*/s32[]{:T(128)}) while((s32[]{:T(128)}, f32[16,1024]{1,0:T(8,128)S(1)}, f32[2,16,1024]{2,1,0:T(8,128)S(1)}, f32[2,16,1024]{2,1,0:T(8,128)S(1)}, ...), condition=%wide.region_2.2_spmd, body=%wide.region_1.1_spmd.sunk | while | flops 212994 | bytes 647333 | solution.py:52
  314.9 21.2 %while.80 = (s32[]{:T(128)}, f32[16,1024]{1,0:T(8,128)S(1)}, f32[2,16,1024]{2,1,0:T(8,128)S(1)}, f32[2,16,1024]{2,1,0:T(8,128)S(1)}, f32[2,16,1024]{2,1,0:T(8,128)}, /*index=5*/s32[]{:T(128)}) while((s32[]{:T(128)}, f32[16,1024]{1,0:T(8,128)S(1)}, f32[2,16,1024]{2,1,0:T(8,128)S(1)}, f32[2,16,1024]{2,1,0:T(8,128)S(1)}, ...), condition=%wide.region_2.2_spmd, body=%wide.region_1.1_spmd.sunk | while | flops 212994 | bytes 647333 | solution.py:52
  344.8 21.2 %while.80 = (s32[]{:T(128)}, f32[16,1024]{1,0:T(8,128)S(1)}, f32[2,16,1024]{2,1,0:T(8,128)S(1)}, f32[2,16,1024]{2,1,0:T(8,128)S(1)}, f32[2,16,1024]{2,1,0:T(8,128)}, /*index=5*/s32[]{:T(128)}) while((s32[]{:T(128)}, f32[16,1024]{1,0:T(8,128)S(1)}, f32[2,16,1024]{2,1,0:T(8,128)S(1)}, f32[2,16,1024]{2,1,0:T(8,128)S(1)}, ...), condition=%wide.region_2.2_spmd, body=%wide.region_1.1_spmd.sunk | while | flops 212994 | bytes 647333 | solution.py:52
  374.7 21.2 %while.80 = (s32[]{:T(128)}, f32[16,1024]{1,0:T(8,128)S(1)}, f32[2,16,1024]{2,1,0:T(8,128)S(1)}, f32[2,16,1024]{2,1,0:T(8,128)S(1)}, f32[2,16,1024]{2,1,0:T(8,128)}, /*index=5*/s32[]{:T(128)}) while((s32[]{:T(128)}, f32[16,1024]{1,0:T(8,128)S(1)}, f32[2,16,1024]{2,1,0:T(8,128)S(1)}, f32[2,16,1024]{2,1,0:T(8,128)S(1)}, ...), condition=%wide.region_2.2_spmd, body=%wide.region_1.1_spmd.sunk | while | flops 212994 | bytes 647333 | solution.py:52
  404.5 21.2 %while.80 = (s32[]{:T(128)}, f32[16,1024]{1,0:T(8,128)S(1)}, f32[2,16,1024]{2,1,0:T(8,128)S(1)}, f32[2,16,1024]{2,1,0:T(8,128)S(1)}, f32[2,16,1024]{2,1,0:T(8,128)}, /*index=5*/s32[]{:T(128)}) while((s32[]{:T(128)}, f32[16,1024]{1,0:T(8,128)S(1)}, f32[2,16,1024]{2,1,0:T(8,128)S(1)}, f32[2,16,1024]{2,1,0:T(8,128)S(1)}, ...), condition=%wide.region_2.2_spmd, body=%wide.region_1.1_spmd.sunk | while | flops 212994 | bytes 647333 | solution.py:52
  434.4 21.2 %while.80 = (s32[]{:T(128)}, f32[16,1024]{1,0:T(8,128)S(1)}, f32[2,16,1024]{2,1,0:T(8,128)S(1)}, f32[2,16,1024]{2,1,0:T(8,128)S(1)}, f32[2,16,1024]{2,1,0:T(8,128)}, /*index=5*/s32[]{:T(128)}) while((s32[]{:T(128)}, f32[16,1024]{1,0:T(8,128)S(1)}, f32[2,16,1024]{2,1,0:T(8,128)S(1)}, f32[2,16,1024]{2,1,0:T(8,128)S(1)}, ...), condition=%wide.region_2.2_spmd, body=%wide.region_1.1_spmd.sunk | while | flops 212994 | bytes 647333 | solution.py:52
  464.3 21.2 %while.80 = (s32[]{:T(128)}, f32[16,1024]{1,0:T(8,128)S(1)}, f32[2,16,1024]{2,1,0:T(8,128)S(1)}, f32[2,16,1024]{2,1,0:T(8,128)S(1)}, f32[2,16,1024]{2,1,0:T(8,128)}, /*index=5*/s32[]{:T(128)}) while((s32[]{:T(128)}, f32[16,1024]{1,0:T(8,128)S(1)}, f32[2,16,1024]{2,1,0:T(8,128)S(1)}, f32[2,16,1024]{2,1,0:T(8,128)S(1)}, ...), condition=%wide.region_2.2_spmd, body=%wide.region_1.1_spmd.sunk | while | flops 212994 | bytes 647333 | solution.py:52
  602.6 418.1 %while.79 = (s32[]{:T(128)}, f32[2,16,1024]{2,1,0:T(8,128)}, f32[16,1024]{1,0:T(8,128)S(1)}, f32[2,16,1024]{2,1,0:T(8,128)S(1)}, f32[2,16,1024]{2,1,0:T(8,128)S(...) while((s32[]{:T(128)}, f32[2,16,1024]{2,1,0:T(8,128)}, ...), condition=%wide.region_8.9_spmd, body=%wide.region_5.8_spmd.sunk | while | flops 360453 | bytes 1827270 | solution.py:98
  610.1 22.7 %while.81 = (s32[]{:T(128)}, f32[16,1024]{1,0:T(8,128)S(1)}, f32[2,16,1024]{2,1,0:T(8,128)S(1)}, f32[2,16,1024]{2,1,0:T(8,128)S(1)}, f32[2,16,1024]{2,1,0:T(8,12...) while((s32[]{:T(128)}, f32[16,1024]{1,0:T(8,128)S(1)}, ...), condition=%wide.region_7.7_spmd, body=%wide.region_6.6_spmd.sunk | while | flops 360451 | bytes 778425 | solution.py:71
  638.3 20.1 %while.81 = (s32[]{:T(128)}, f32[16,1024]{1,0:T(8,128)S(1)}, f32[2,16,1024]{2,1,0:T(8,128)S(1)}, f32[2,16,1024]{2,1,0:T(8,128)S(1)}, f32[2,16,1024]{2,1,0:T(8,12...) while((s32[]{:T(128)}, f32[16,1024]{1,0:T(8,128)S(1)}, ...), condition=%wide.region_7.7_spmd, body=%wide.region_6.6_spmd.sunk | while | flops 360451 | bytes 778425 | solution.py:71
  664.1 20.1 %while.81 = (s32[]{:T(128)}, f32[16,1024]{1,0:T(8,128)S(1)}, f32[2,16,1024]{2,1,0:T(8,128)S(1)}, f32[2,16,1024]{2,1,0:T(8,128)S(1)}, f32[2,16,1024]{2,1,0:T(8,12...) while((s32[]{:T(128)}, f32[16,1024]{1,0:T(8,128)S(1)}, ...), condition=%wide.region_7.7_spmd, body=%wide.region_6.6_spmd.sunk | while | flops 360451 | bytes 778425 | solution.py:71
  689.9 20.1 %while.81 = (s32[]{:T(128)}, f32[16,1024]{1,0:T(8,128)S(1)}, f32[2,16,1024]{2,1,0:T(8,128)S(1)}, f32[2,16,1024]{2,1,0:T(8,128)S(1)}, f32[2,16,1024]{2,1,0:T(8,12...) while((s32[]{:T(128)}, f32[16,1024]{1,0:T(8,128)S(1)}, ...), condition=%wide.region_7.7_spmd, body=%wide.region_6.6_spmd.sunk | while | flops 360451 | bytes 778425 | solution.py:71
  715.8 20.1 %while.81 = (s32[]{:T(128)}, f32[16,1024]{1,0:T(8,128)S(1)}, f32[2,16,1024]{2,1,0:T(8,128)S(1)}, f32[2,16,1024]{2,1,0:T(8,128)S(1)}, f32[2,16,1024]{2,1,0:T(8,12...) while((s32[]{:T(128)}, f32[16,1024]{1,0:T(8,128)S(1)}, ...), condition=%wide.region_7.7_spmd, body=%wide.region_6.6_spmd.sunk | while | flops 360451 | bytes 778425 | solution.py:71
  741.6 20.1 %while.81 = (s32[]{:T(128)}, f32[16,1024]{1,0:T(8,128)S(1)}, f32[2,16,1024]{2,1,0:T(8,128)S(1)}, f32[2,16,1024]{2,1,0:T(8,128)S(1)}, f32[2,16,1024]{2,1,0:T(8,12...) while((s32[]{:T(128)}, f32[16,1024]{1,0:T(8,128)S(1)}, ...), condition=%wide.region_7.7_spmd, body=%wide.region_6.6_spmd.sunk | while | flops 360451 | bytes 778425 | solution.py:71
  767.4 20.1 %while.81 = (s32[]{:T(128)}, f32[16,1024]{1,0:T(8,128)S(1)}, f32[2,16,1024]{2,1,0:T(8,128)S(1)}, f32[2,16,1024]{2,1,0:T(8,128)S(1)}, f32[2,16,1024]{2,1,0:T(8,12...) while((s32[]{:T(128)}, f32[16,1024]{1,0:T(8,128)S(1)}, ...), condition=%wide.region_7.7_spmd, body=%wide.region_6.6_spmd.sunk | while | flops 360451 | bytes 778425 | solution.py:71
  793.3 20.1 %while.81 = (s32[]{:T(128)}, f32[16,1024]{1,0:T(8,128)S(1)}, f32[2,16,1024]{2,1,0:T(8,128)S(1)}, f32[2,16,1024]{2,1,0:T(8,128)S(1)}, f32[2,16,1024]{2,1,0:T(8,12...) while((s32[]{:T(128)}, f32[16,1024]{1,0:T(8,128)S(1)}, ...), condition=%wide.region_7.7_spmd, body=%wide.region_6.6_spmd.sunk | while | flops 360451 | bytes 778425 | solution.py:71
  819.1 20.1 %while.81 = (s32[]{:T(128)}, f32[16,1024]{1,0:T(8,128)S(1)}, f32[2,16,1024]{2,1,0:T(8,128)S(1)}, f32[2,16,1024]{2,1,0:T(8,128)S(1)}, f32[2,16,1024]{2,1,0:T(8,12...) while((s32[]{:T(128)}, f32[16,1024]{1,0:T(8,128)S(1)}, ...), condition=%wide.region_7.7_spmd, body=%wide.region_6.6_spmd.sunk | while | flops 360451 | bytes 778425 | solution.py:71
  845.0 20.1 %while.81 = (s32[]{:T(128)}, f32[16,1024]{1,0:T(8,128)S(1)}, f32[2,16,1024]{2,1,0:T(8,128)S(1)}, f32[2,16,1024]{2,1,0:T(8,128)S(1)}, f32[2,16,1024]{2,1,0:T(8,12...) while((s32[]{:T(128)}, f32[16,1024]{1,0:T(8,128)S(1)}, ...), condition=%wide.region_7.7_spmd, body=%wide.region_6.6_spmd.sunk | while | flops 360451 | bytes 778425 | solution.py:71
  870.8 20.1 %while.81 = (s32[]{:T(128)}, f32[16,1024]{1,0:T(8,128)S(1)}, f32[2,16,1024]{2,1,0:T(8,128)S(1)}, f32[2,16,1024]{2,1,0:T(8,128)S(1)}, f32[2,16,1024]{2,1,0:T(8,12...) while((s32[]{:T(128)}, f32[16,1024]{1,0:T(8,128)S(1)}, ...), condition=%wide.region_7.7_spmd, body=%wide.region_6.6_spmd.sunk | while | flops 360451 | bytes 778425 | solution.py:71
  896.6 20.1 %while.81 = (s32[]{:T(128)}, f32[16,1024]{1,0:T(8,128)S(1)}, f32[2,16,1024]{2,1,0:T(8,128)S(1)}, f32[2,16,1024]{2,1,0:T(8,128)S(1)}, f32[2,16,1024]{2,1,0:T(8,12...) while((s32[]{:T(128)}, f32[16,1024]{1,0:T(8,128)S(1)}, ...), condition=%wide.region_7.7_spmd, body=%wide.region_6.6_spmd.sunk | while | flops 360451 | bytes 778425 | solution.py:71
  922.5 20.1 %while.81 = (s32[]{:T(128)}, f32[16,1024]{1,0:T(8,128)S(1)}, f32[2,16,1024]{2,1,0:T(8,128)S(1)}, f32[2,16,1024]{2,1,0:T(8,128)S(1)}, f32[2,16,1024]{2,1,0:T(8,12...) while((s32[]{:T(128)}, f32[16,1024]{1,0:T(8,128)S(1)}, ...), condition=%wide.region_7.7_spmd, body=%wide.region_6.6_spmd.sunk | while | flops 360451 | bytes 778425 | solution.py:71
  974.2 20.1 %while.81 = (s32[]{:T(128)}, f32[16,1024]{1,0:T(8,128)S(1)}, f32[2,16,1024]{2,1,0:T(8,128)S(1)}, f32[2,16,1024]{2,1,0:T(8,128)S(1)}, f32[2,16,1024]{2,1,0:T(8,12...) while((s32[]{:T(128)}, f32[16,1024]{1,0:T(8,128)S(1)}, ...), condition=%wide.region_7.7_spmd, body=%wide.region_6.6_spmd.sunk | while | flops 360451 | bytes 778425 | solution.py:71
  (853 shorter events, 1054.5 us)
Async XLA Ops:
  2.2 8.1 collective-permute-start.5
  10.4 9.6 collective-permute-start.3
  18.0 7.6 collective-permute-start.4
  37.9 8.0 collective-permute-start.5
  58.5 7.6 collective-permute-start.4
  67.8 8.0 collective-permute-start.5
  77.8 7.6 collective-permute-start.4
  97.7 8.0 collective-permute-start.5
  127.6 8.0 collective-permute-start.5
  137.6 7.6 collective-permute-start.4
  157.5 8.0 collective-permute-start.5
  187.4 8.0 collective-permute-start.5
  197.3 7.6 collective-permute-start.4
  217.2 8.0 collective-permute-start.5
  247.1 8.0 collective-permute-start.5
  257.1 7.6 collective-permute-start.4
  277.0 8.0 collective-permute-start.5
  306.9 8.0 collective-permute-start.5
  316.9 7.6 collective-permute-start.4
  327.5 7.6 collective-permute-start.4
  336.8 8.0 collective-permute-start.5
  366.7 8.0 collective-permute-start.5
  387.2 7.6 collective-permute-start.4
  396.5 8.0 collective-permute-start.5
  426.4 8.0 collective-permute-start.5
  447.0 7.6 collective-permute-start.4
  456.3 8.0 collective-permute-start.5
  488.7 13.2 %collective-permute-start.6 = (f32[6,1,16,1024]{3,0,2,1:T(8,128)}, f32[6,1,16,1024]{3,0,2,1:T(8,128)S(1)}, u32[]{:S(2)}, u32[]{:S(2)}) collective-permute-start(f32[6,1,16,1024]{3,0,2,1:T(8,128)} %get-tuple-element.570), channel_id=1, source_target_pairs={{0,16},{16,32},{32,48},{48,64},{64,80},{80,96},{96,112},{112,128},... | collective-permute-start | bytes 1179656 | tf_op jit(solution)/shard_map/ppermute | solution.py:21
  490.7 13.0 %collective-permute-start.7 = (f32[6,1,16,1024]{3,0,2,1:T(8,128)}, f32[6,1,16,1024]{3,0,2,1:T(8,128)S(1)}, u32[]{:S(2)}, u32[]{:S(2)}) collective-permute-start(f32[6,1,16,1024]{3,0,2,1:T(8,128)} %get-tuple-element.571), channel_id=1, source_target_pairs={{16,0},{32,16},{48,32},{64,48},{80,64},{96,80},{112,96},{128,112},... | collective-permute-start | bytes 1179656 | tf_op jit(solution)/shard_map/ppermute | solution.py:22
  504.4 11.8 %collective-permute-start.8 = (f32[6,4,1,1024]{3,0,2,1:T(8,128)}, f32[6,4,1,1024]{3,0,2,1:T(8,128)S(1)}, u32[]{:S(2)}, u32[]{:S(2)}) collective-permute-start(f32[6,4,1,1024]{3,0,2,1:T(8,128)} %get-tuple-element.568), channel_id=1, source_target_pairs={{0,1},{1,2},{2,3},{3,4},{4,5},{5,6},{6,7},{7,8},{8,9},{9,10},{10,1... | collective-permute-start | bytes 294920 | tf_op jit(solution)/shard_map/ppermute | solution.py:21
  506.4 9.9 collective-permute-start.9
  625.0 7.6 collective-permute-start.1
  (170 other events, 1387.1 us)
where the time goes:
time: 1040 us; the launch traced here: 1020 us
  starting transfers between devices  478 us (46%)
  waiting for transfers between devices  381 us (37%)
  matrix products  80.7 us (8%)
  other arithmetic  44 us (4%)
  local copies, waits for them, and re-layouts  30.9 us (3%)
    ppermute x66, waiting for transfers between devices, extended(): before = lax.ppermute(last, axis, up)  252 us
    ppermute x66, starting transfers between devices, extended(): before = lax.ppermute(last, axis, up)  241 us
    ppermute x66, starting transfers between devices, extended(): after = lax.ppermute(initial, axis, down)  153 us
    ppermute x32, waiting for transfers between devices, from_behind(): return lax.ppermute(block, axis, route)  127 us
    ppermute x32, starting transfers between devices, from_behind(): return lax.ppermute(block, axis, route)  83.2 us
    dot_general x54, matrix products, apply_blocks(): jnp.einsum('cd,dzxy->czxy', matrix, shifted, precision=highest)  80.5 us
    dynamic_update_slice x96, other arithmetic, forward_block(): _, (printed, support) = lax.scan(forward_layer, bottom, design)  36 us
  transfers between devices with their start and end apart: 164, of which 98 were waited for; matrix products, arithmetic and copies ran while one was open for 1% of the time, Pallas kernels for 0%

commit v1 on v0

v1 whole, which is shorter than its diff:
```python
import functools

import jax
import jax.numpy as jnp
from jax import lax
from jax.experimental import pallas as pl
from jax.experimental.pallas import tpu as pltpu
from jax.sharding import PartitionSpec as P

smooth_eps = 0.0001
root_eps = 0.01
base_floor = 0.05
modulus_floor = 0.001
f32 = jnp.float32
bf16 = jnp.bfloat16
VM = pl.BlockSpec(memory_space=pltpu.VMEM)
SM = pl.BlockSpec(memory_space=pltpu.SMEM)


def call(kernel, outs, args, scratch=(), smem=0, cost=2000000):
    specs = [SM] * smem + [VM] * (len(args) - smem)
    return pl.pallas_call(
        kernel,
        out_shape=[jax.ShapeDtypeStruct(s, d) for s, d in outs],
        in_specs=specs,
        out_specs=[VM] * len(outs),
        scratch_shapes=list(scratch),
        cost_estimate=pl.CostEstimate(flops=cost, bytes_accessed=cost, transcendentals=0),
    )(*args)


def lane(shape):
    return lax.broadcasted_iota(jnp.int32, shape, len(shape) - 1)


def row(shape):
    return lax.broadcasted_iota(jnp.int32, shape, len(shape) - 2)


def shifted_tiles(x):
    tiles = x.shape[1] // 128
    moved = pltpu.roll(x, 32, 1)
    cut = [moved[:, 128 * t : 128 * t + 128] for t in range(tiles)]
    low = lane(cut[0].shape) < 32
    zero = jnp.zeros_like(cut[0])
    return (
        [zero, jnp.where(low, zero, cut[0])]
        + cut[1:]
        + [jnp.where(low, cut[0], zero), zero]
    )


def prepare_density(dens_ref, out_ref):
    x = dens_ref[...].reshape(32, 1024)
    s = shifted_tiles(x)
    w = [pltpu.roll(t, 64, 1) for t in s]
    low = lane(s[0].shape) < 64
    for p in range(16):
        k = p // 2 + 1
        if p % 2 == 0:
            first, second = s[k], jnp.where(low, s[k + 1], s[k - 1])
        else:
            first, second = jnp.where(low, w[k], w[k + 1]), jnp.where(low, w[k + 1], w[k])
        out_ref[p, :, :, 0:128] = first.reshape(2, 16, 128)
        out_ref[p, :, :, 128:256] = second.reshape(2, 16, 128)


def prepare_fields(pq_ref, disp_ref, adj_ref, mask_ref, out_ref, base_ref, wide_ref):
    for number, ref in ((0, disp_ref), (3, adj_ref)):
        for c in range(3):
            s = shifted_tiles(ref[c].reshape(32, 1024))
            w = [pltpu.roll(t, 64, 1) for t in s]
            low = lane(s[0].shape) < 64
            for p in range(16):
                k = p // 2 + 1
                first = s[k] if p % 2 == 0 else jnp.where(low, w[k], w[k + 1])
                out_ref[p, number + c] = first.reshape(2, 16, 128)
    base = base_floor + (1.0 - base_floor) * mask_ref[...].astype(f32)
    for t, tile in enumerate(shifted_tiles(base)):
        wide_ref[:, 128 * t : 128 * t + 128] = tile
    p = pq_ref[0]
    k = lax.div(p, 2)
    odd = (p - 2 * k).astype(f32)
    before, here, after = [wide_ref[:, pl.ds(pl.multiple_of((k + t) * 128, 128), 128)] for t in range(3)]
    here2, after2 = pltpu.roll(here, 64, 1), pltpu.roll(after, 64, 1)
    low = lane(here.shape) < 64
    even0, even1 = here, jnp.where(low, after, before)
    odd0, odd1 = jnp.where(low, here2, after2), jnp.where(low, after2, here2)
    base_ref[:, 0:128] = even0 * (1.0 - odd) + odd0 * odd
    base_ref[:, 128:256] = even1 * (1.0 - odd) + odd1 * odd


def matrices(pattern_ref, blocks_ref, out_ref):
    k = lane((8, 256))
    dk = jnp.where(k < 192, k >> 6, (k - 192) >> 3)
    zk = jnp.where(k < 192, (k >> 4) & 3, ((k - 192) >> 1) & 3)
    at = [[(dk == d) & (zk == z) for z in range(4)] for d in range(3)]
    k2 = lane((16, 256))
    xk = jnp.where(k2 < 192, k2 & 15, jnp.where((k2 & 1) == 0, -1, 16))
    step = xk - row((16, 256))
    for kind in range(2):
        for ds in (-1, 0, 1):
            for c in range(3):
                rows = [[None] * 3, [None] * 3]
                for db in (-1, 0, 1):
                    values = {}
                    for da in (-1, 0, 1):
                        sign = -1 if kind == 0 else 1
                        o = 9 * (sign * da + 1) + 3 * (sign * db + 1) + (sign * ds + 1)
                        start = pattern_ref[o] * 9
                        for d in range(3):
                            values[da, d] = blocks_ref[start + (d * 3 + c if kind == 0 else c * 3 + d)]
                    for zi in range(2):
                        r = jnp.zeros((8, 256), f32)
                        for da in (-1, 0, 1):
                            for d in range(3):
                                r = jnp.where(at[d][da + 1 + zi], values[da, d], r)
                        rows[zi][db + 1] = r
                for zi in range(2):
                    m = jnp.zeros((16, 256), f32)
                    for db in (-1, 0, 1):
                        r = rows[zi][db + 1]
                        m = jnp.where(step == db, jnp.concatenate([r, r], 0), m)
                    high = m.astype(bf16)
                    low = (m - high.astype(f32)).astype(bf16)
                    start = ((ds + 1) * 6 + c * 2 + zi) * 16
                    out_ref[2 * kind, start : start + 16] = high
                    out_ref[2 * kind + 1, start : start + 16] = low


def pack_density(dens_ref, base_ref, up_ref, down_ref):
    up_ref[0:16] = base_ref[...]
    down_ref[0:16] = base_ref[...]
    for ph in range(2):
        for j in range(15):
            x = dens_ref[16 * ph + j]
            if j < 7:
                start = 16 + ph * 176 + j * 16
                up_ref[start : start + 16] = x
                down_ref[start : start + 16] = x
            else:
                start = 16 + ph * 176 + 112 + (j - 7) * 8
                up_ref[start : start + 8] = x[0:8]
                down_ref[start : start + 8] = x[8:16]


def cross_of(x):
    rows, width = x.shape
    return (
        x
        + pltpu.roll(x, 1, 0)
        + pltpu.roll(x, rows - 1, 0)
        + pltpu.roll(x, 1, 1)
        + pltpu.roll(x, width - 1, 1)
    )


def forward(ph, pq_ref, dens_ref, upper_ref, lower_ref, own_ref, *refs):
    if ph == 0:
        up, down = upper_ref[0:16], lower_ref[0:16]
        printed_ref, support_ref, state_ref = refs
    else:
        su_ref, sd_ref, printed_ref, support_ref, state_ref = refs
        up, down = su_ref[...], sd_ref[...]
    p, q = pq_ref[0], pq_ref[1]
    current = jnp.concatenate([up, own_ref[...], down], 0)
    l = lane((48, 256))
    y = 64 * p - 32 + l - jnp.where(l < 192, 0, 256)
    x = 16 * q - 16 + row((48, 256))
    inside = jnp.where((x >= 0) & (x < 256) & (y >= 0) & (y < 1024), 1.0, 0.0)
    rows = 48
    for j in range(16):
        p2 = current * current
        p4 = p2 * p2
        p8 = p4 * p4
        edge = (48 - rows) // 2
        cross = cross_of(p8 * p8 * inside[edge : 48 - edge])
        count = 48 if j < 7 else (32 if j < 15 else 16)
        if count < rows:
            cross = cross[8 : rows - 8]
        rows = count
        design = dens_ref[16 * ph + j]
        if j < 15:
            size = 16 if j < 7 else 8
            start = 16 + ph * 176 + (j * 16 if j < 7 else 112 + (j - 7) * 8)
            design = jnp.concatenate(
                [upper_ref[start : start + size], design, lower_ref[start : start + size]], 0
            )
        support = jnp.sqrt(jnp.sqrt(jnp.sqrt(jnp.sqrt(cross))))
        differ = design - support
        current = 0.5 * (design + support - jnp.sqrt(differ * differ + smooth_eps) + root_eps)
        edge = (rows - 16) // 2
        printed_ref[j] = current[edge : edge + 16, 0:128]
        support_ref[j] = support[edge : edge + 16, 0:128]
    state_ref[...] = current


def pack_rows(fields_ref, up_ref, down_ref):
    for c in range(3):
        for z in range(32):
            x = fields_ref[z // 2, 3 + c, z % 2]
            up_ref[c * 32 + z : c * 32 + z + 1] = x[0:1]
            down_ref[c * 32 + z : c * 32 + z + 1] = x[15:16]


def fill_halo(halo, upper, lower):
    halo[...] = jnp.zeros(halo.shape, f32)
    for c in range(3):
        halo[c, pl.ds(2, 32, stride=2)] = upper[c * 32 : c * 32 + 32]
        halo[c, pl.ds(3, 32, stride=2)] = lower[c * 32 : c * 32 + 32]


def product(field, halo, mat_ref, kind, i):
    edges = [halo[d, pl.ds(pl.multiple_of(8 * i, 8), 16)] for d in range(3)]
    sides = []
    for pair in range(2):
        main = [field[d, pl.ds(4 * i + 2 * pair, 4)].reshape(64, 128) for d in range(3)]
        rim = [e[4 * pair : 4 * pair + 8] for e in edges]
        sides.append(jnp.concatenate(main + rim + [jnp.zeros((40, 128), f32)], 0))
    u = jnp.concatenate(sides, 1)
    high = u.astype(bf16)
    low = (u - high.astype(f32)).astype(bf16)
    dot = functools.partial(jnp.dot, preferred_element_type=f32)
    mat_high, mat_low = mat_ref[2 * kind], mat_ref[2 * kind + 1]
    out = dot(mat_high, high) + dot(mat_high, low) + dot(mat_low, high)

    def pick(pair, c, zi):
        parts = [
            out[(s * 6 + c * 2 + zi) * 16 : (s * 6 + c * 2 + zi) * 16 + 16, 128 * pair : 128 * pair + 128]
            for s in range(3)
        ]
        return parts[1] + pltpu.roll(parts[0], 1, 1) + pltpu.roll(parts[2], 127, 1)

    return pick


def edges_of(pq_ref):
    q = pq_ref[1]
    return jnp.where(q > 0, 1.0, 0.0), jnp.where(q < 15, 1.0, 0.0)


def direct_part(pq_ref, fields_ref, upper_ref, lower_ref, mat_ref, out_ref, field, halo):
    keep_up, keep_down = edges_of(pq_ref)
    fill_halo(halo, upper_ref[...] * keep_up, lower_ref[...] * keep_down)
    for c in range(3):
        field[c, 0] = jnp.zeros((16, 128), f32)
        field[c, 33] = jnp.zeros((16, 128), f32)
        for z in range(32):
            field[c, z + 1] = fields_ref[z // 2, 3 + c, z % 2]

    def body(i, carry):
        pick = product(field, halo, mat_ref, 0, i)
        for pair in range(2):
            for zi in range(2):
                total = fields_ref[2 * i + pair, 0, zi] * pick(pair, 0, zi)
                for c in (1, 2):
                    total = total + fields_ref[2 * i + pair, c, zi] * pick(pair, c, zi)
                out_ref[4 * i + 2 * pair + zi] = total
        return carry

    lax.fori_loop(0, 8, body, 0)


def coefficients(pq_ref, p0_ref, s0_ref, p1_ref, s1_ref, dens_ref, d0_ref, fields_ref, *refs):
    a_ref, b_ref, e_ref, f_ref, up_ref, down_ref = refs
    y = 64 * pq_ref[0] - 32 + lane((16, 128))
    inside = (y >= 0) & (y < 1024)
    for z in range(32):
        ph, j = divmod(z, 16)
        printed = (p0_ref, p1_ref)[ph][j]
        support = (s0_ref, s1_ref)[ph][j]
        design = dens_ref[z, :, 0:128]
        p2 = printed * printed
        p3 = p2 * printed
        modulus = modulus_floor + (1.0 - modulus_floor) * p3
        p6 = p3 * p3
        p15 = p6 * p6 * p3
        s2 = support * support
        s3 = s2 * support
        s6 = s3 * s3
        s15 = s6 * s6 * s3
        differ = design - support
        slope = differ / jnp.sqrt(differ * differ + smooth_eps)
        direct = d0_ref[z] * (3.0 * (1.0 - modulus_floor)) * p2
        gain = 0.5 * (1.0 + slope) / s15
        kept = 0.5 * (1.0 - slope)
        zero = jnp.zeros_like(direct)
        a = jnp.where(inside, direct * gain, zero)
        b = jnp.where(inside, p15 * gain, zero)
        a_ref[z] = a
        b_ref[z] = b
        e_ref[z] = direct * kept
        f_ref[z] = p15 * kept
        for number, value in ((0, a), (1, b)):
            start = (number * 2 + ph) * 176
            if 1 <= j <= 8:
                start += (j - 1) * 8
                up_ref[start : start + 8] = value[0:8]
                down_ref[start : start + 8] = value[8:16]
            elif j >= 9:
                start += 64 + (j - 9) * 16
                up_ref[start : start + 16] = value
                down_ref[start : start + 16] = value
        for c in range(3):
            u = modulus * fields_ref[z // 2, c, z % 2]
            start = 704 + c * 32 + z
            up_ref[start : start + 1] = u[0:1]
            down_ref[start : start + 1] = u[15:16]


def force_part(pq_ref, p0_ref, p1_ref, fields_ref, upper_ref, lower_ref, mat_ref, out_ref, field, halo):
    keep_up, keep_down = edges_of(pq_ref)
    fill_halo(halo, upper_ref[704:800] * keep_up, lower_ref[704:800] * keep_down)
    for c in range(3):
        field[c, 0] = jnp.zeros((16, 128), f32)
        field[c, 33] = jnp.zeros((16, 128), f32)
    for z in range(32):
        printed = (p0_ref, p1_ref)[z // 16][z % 16]
        modulus = modulus_floor + (1.0 - modulus_floor) * (printed * printed * printed)
        for c in range(3):
            field[c, z + 1] = modulus * fields_ref[z // 2, c, z % 2]

    def body(i, carry):
        pick = product(field, halo, mat_ref, 1, i)
        low = lane((16, 128)) < 64
        for pair in range(2):
            for c in range(3):
                first = pltpu.roll(pick(pair, c, 0), 96, 1)
                second = pltpu.roll(pick(pair, c, 1), 32, 1)
                out_ref[2 * i + pair, c] = jnp.where(low, first, second)
        return carry

    lax.fori_loop(0, 8, body, 0)


def backward(ph, pq_ref, a_ref, b_ref, e_ref, f_ref, upper_ref, lower_ref, *refs):
    keep_up, keep_down = edges_of(pq_ref)
    if ph == 1:
        sens_ref, state_ref = refs
        current = None
    else:
        own_ref, su_ref, sd_ref, sens1_ref, force_ref, out_ref = refs
        current = jnp.concatenate([su_ref[...] * keep_up, own_ref[...], sd_ref[...] * keep_down], 0)
    rows = 48
    low = lane((16, 128)) < 64
    later = None
    for j in range(15, -1, -1):
        z = 16 * ph + j
        count = 48 if j >= 9 else (32 if j >= 1 else 16)
        sens = e_ref[z]
        coef = []
        for number, ref in ((0, a_ref), (1, b_ref)):
            value = ref[z]
            if j >= 1:
                size = 8 if j <= 8 else 16
                start = (number * 2 + ph) * 176 + ((j - 1) * 8 if j <= 8 else 64 + (j - 9) * 16)
                value = jnp.concatenate(
                    [
                        upper_ref[start : start + size] * keep_up,
                        value,
                        lower_ref[start : start + size] * keep_down,
                    ],
                    0,
                )
            coef.append(value)
        if current is None:
            current = coef[0]
        else:
            cross = cross_of(current)
            edge = (rows - 16) // 2
            sens = sens + f_ref[z] * cross[edge : edge + 16]
            if count < rows:
                cross = cross[8 : rows - 8]
            current = coef[0] + coef[1] * cross
        rows = count
        if j % 2 == 1:
            later = pltpu.roll(sens, 32, 1)
        else:
            packed = jnp.where(low, pltpu.roll(sens, 96, 1), later)
            if ph == 1:
                sens_ref[j // 2] = packed
            else:
                out_ref[j // 2, 3] = packed
    if ph == 1:
        state_ref[...] = current
    else:
        out_ref[:, 0:3] = force_ref[...]
        for i in range(8):
            out_ref[8 + i, 3] = sens1_ref[i]


def unpack(in_ref, force_ref, sens_ref):
    low = lane((16, 128)) < 64
    for k in range(8):
        for c in range(4):
            first, second = in_ref[2 * k, c], in_ref[2 * k + 1, c]
            layers = (
                jnp.where(low, first, pltpu.roll(second, 64, 1)),
                jnp.where(low, pltpu.roll(first, 64, 1), second),
            )
            for i in range(2):
                if c < 3:
                    force_ref[c, i, :, 128 * k : 128 * k + 128] = layers[i]
                else:
                    sens_ref[i, :, 128 * k : 128 * k + 128] = layers[i]


def trade(to_lower, to_upper):
    count = lax.axis_size("lat")
    up = [(i, (i + 1) % count) for i in range(count)]
    down = [(j, i) for i, j in up]
    return lax.ppermute(to_lower, "lat", up), lax.ppermute(to_upper, "lat", down)


def exchange(x):
    return lax.all_to_all(x, "build", 0, 0, tiled=True)


def on_device(density, support_mask, pattern, blocks, displacement, adjoint):
    pq = jnp.stack([lax.axis_index("build"), lax.axis_index("lat")]).astype(jnp.int32)
    (windows,) = call(prepare_density, [((16, 2, 16, 256), f32)], [density])
    dens = exchange(windows).reshape(32, 16, 256)
    fields, base = call(
        prepare_fields,
        [((16, 6, 2, 16, 128), f32), ((16, 256), f32)],
        [pq, displacement, adjoint, support_mask],
        scratch=[pltpu.VMEM((16, 11 * 128), f32)],
        smem=1,
    )
    (mats,) = call(matrices, [((4, 288, 256), bf16)], [pattern, blocks.reshape(72)], smem=2)
    fields = exchange(fields)
    up_send, down_send = call(pack_density, [((368, 256), f32)] * 2, [dens, base])
    upper, lower = trade(down_send, up_send)
    layer = ((16, 16, 128), f32)
    p0, s0, state = call(
        functools.partial(forward, 0),
        [layer, layer, ((16, 256), f32)],
        [pq, dens, upper, lower, base],
        smem=1,
    )
    state_up, state_down = trade(state, state)
    p1, s1, _ = call(
        functools.partial(forward, 1),
        [layer, layer, ((16, 256), f32)],
        [pq, dens, upper, lower, state, state_up, state_down],
        smem=1,
    )
    up_send, down_send = call(pack_rows, [((96, 128), f32)] * 2, [fields])
    adj_up, adj_down = trade(down_send, up_send)
    work = [pltpu.VMEM((3, 34, 16, 128), f32), pltpu.VMEM((3, 72, 128), f32)]
    (d0,) = call(
        direct_part,
        [((32, 16, 128), f32)],
        [pq, fields, adj_up, adj_down, mats],
        scratch=work,
        smem=1,
    )
    whole = ((32, 16, 128), f32)
    a, b, e, f, up_send, down_send = call(
        coefficients,
        [whole] * 4 + [((800, 128), f32)] * 2,
        [pq, p0, s0, p1, s1, dens, d0, fields],
        smem=1,
    )
    upper, lower = trade(down_send, up_send)
    sens1, state = call(
        functools.partial(backward, 1),
        [((8, 16, 128), f32), ((16, 128), f32)],
        [pq, a, b, e, f, upper, lower],
        smem=1,
    )
    state_up, state_down = trade(state, state)
    (force,) = call(
        force_part,
        [((16, 3, 16, 128), f32)],
        [pq, p0, p1, fields, upper, lower, mats],
        scratch=work,
        smem=1,
    )
    (packed,) = call(
        functools.partial(backward, 0),
        [((16, 4, 16, 128), f32)],
        [pq, a, b, e, f, upper, lower, state, state_up, state_down, sens1, force],
        smem=1,
    )
    packed = exchange(packed)
    return tuple(call(unpack, [((3, 2, 16, 1024), f32), ((2, 16, 1024), f32)], [packed]))


def solution(mesh):
    in_specs = (
        P("build", "lat", None),
        P("lat", None),
        P(),
        P(),
        P(None, "build", "lat", None),
        P(None, "build", "lat", None),
    )
    out_specs = (P(None, "build", "lat", None), P("build", "lat", None))
    return jax.shard_map(
        on_device, mesh=mesh, in_specs=in_specs, out_specs=out_specs, check_vma=False
    )
```

time: 1040 us -> 144 us (0.14)
  the two profiles are of different devices: /device:TPU:12 before, /device:TPU:1 now
where the time goes in v1:
time: 144 us; the launch traced here: 143 us
  Pallas kernels  43 us (30%)
  waiting for transfers between devices  38.8 us (27%)
  starting transfers between devices  32.7 us (23%)
  blocking collectives  19.7 us (14%)
  local copies, waits for them, and re-layouts  7.5 us (5%)
    pallas_call x13, Pallas kernels, call(): pl.pallas_call(kernel, out_shape=[jax.ShapeDtypeStruct(s, d) for s, d in...  43 us
    all_to_all x2, waiting for transfers between devices, exchange(): return lax.all_to_all(x, 'build', 0, 0, tiled=True)  28.8 us
    all_to_all x1, blocking collectives, exchange(): return lax.all_to_all(x, 'build', 0, 0, tiled=True)  19.7 us
    ppermute x5, starting transfers between devices, trade(): lax.ppermute(to_upper, 'lat', down)  17.9 us
    all_to_all x2, starting transfers between devices, exchange(): return lax.all_to_all(x, 'build', 0, 0, tiled=True)  13.2 us
    ppermute x5, waiting for transfers between devices, trade(): lax.ppermute(to_lower, 'lat', up)  9.99 us
    unnamed x27, local copies, waits for them, and re-layouts  6.87 us
  transfers between devices with their start and end apart: 12, of which 4 were waited for; matrix products, arithmetic and copies ran while one was open for 1% of the time, Pallas kernels for 17%

profile of v1, /device:TPU:1, one launch (start us, length us, event | category | flops | bytes accessed | tf_op | source)
XLA Modules:
  0.0 142.9 jit_solution(13757480387578859035)
XLA Ops:
  0.6 1.9 %shard_map.77 = f32[16,2,16,256]{3,2,1,0:T(8,128)} custom-call(f32[2,16,1024]{2,1,0:T(8,128)} %dens_ref.1), custom_call_target="tpu_custom_call" | custom-call | flops 2000000 | bytes 2000000 | tf_op jit(solution)/shard_map/pallas_call | solution.py:22
  2.5 8.4 %all-to-all-start = ((f32[16,2,16,256]{3,2,1,0:T(8,128)}), f32[16,2,16,256]{3,2,1,0:T(8,128)S(1)}, u32[]{:S(2)}, u32[]{:S(2)}) async-start(f32[16,2,16,256]{3,2,1,0:T(8,128)} %shard_map.77), calls=%async_computation | async-start | bytes 1048576 | tf_op jit(solution)/shard_map/all_to_all | solution.py:416
  11.5 3.2 %shard_map.78 = (f32[16,6,2,16,128]{4,3,2,1,0:T(8,128)}, f32[16,256]{1,0:T(8,128)}) custom-call(s32[2]{0:T(128)} %pad_add_fusion.pq_ref, f32[3,2,16,1024]{3,2,1,0:T(8,128)} %disp_ref.1, f32[3,2,16,1024]{3,2,1,0:T(8,128)} %adj_ref.1, s32[16,1024]{1,0:T(8,128)} %mask_ref.1), custom_call_target="tpu_custom_call" | custom-call | flops 2000000 | bytes 2000000 | tf_op jit(solution)/shard_map/pallas_call | solution.py:22
  14.7 7.5 %all-to-all-done = f32[16,2,16,256]{3,2,1,0:T(8,128)S(1)} async-done(((f32[16,2,16,256]{3,2,1,0:T(8,128)}), f32[16,2,16,256]{3,2,1,0:T(8,128)S(1)}, u32[]{:S(2)}, u32[]{:S(2)}) %all-to-all-start) | async-done | bytes 524320 | tf_op jit(solution)/shard_map/all_to_all | solution.py:416
  22.1 0.8 copy-done.1
  22.9 4.7 %all-to-all-start.1 = ((f32[16,6,2,16,128]{4,3,2,1,0:T(8,128)}), f32[16,6,2,16,128]{4,3,2,1,0:T(8,128)S(1)}, u32[]{:S(2)}, u32[]{:S(2)}) async-start(f32[16,6,2,16,128]{4,3,2,1,0:T(8,128)} %get-tuple-element.29), calls=%async_computation.1 | async-start | bytes 3145728 | tf_op jit(solution)/shard_map/all_to_all | solution.py:416
  27.7 2.0 %shard_map.79 = (f32[368,256]{1,0:T(8,128)}, f32[368,256]{1,0:T(8,128)}) custom-call(f32[32,16,256]{2,1,0:T(8,128)} %bitcast.3, f32[16,256]{1,0:T(8,128)} %get-tuple-element.21.base_ref.own_ref), custom_call_target="tpu_custom_call" | custom-call | flops 2000000 | bytes 2000000 | tf_op jit(solution)/shard_map/pallas_call | solution.py:22
  29.6 1.6 %collective-permute-start = (f32[368,256]{1,0:T(8,128)}, f32[368,256]{1,0:T(8,128)S(1)}, u32[]{:S(2)}, u32[]{:S(2)}) collective-permute-start(f32[368,256]{1,0:T(8,128)} %get-tuple-element.22), channel_id=1, source_target_pairs={{0,1},{1,2},{2,3},{3,4},{4,5},{5,6},{6,7},{7,8},{8,9},{9,10},{10,1... | collective-permute-start | bytes 1130504 | tf_op jit(solution)/shard_map/ppermute | solution.py:412
  31.3 4.1 %collective-permute-start.1 = (f32[368,256]{1,0:T(8,128)}, f32[368,256]{1,0:T(8,128)S(1)}, u32[]{:S(2)}, u32[]{:S(2)}) collective-permute-start(f32[368,256]{1,0:T(8,128)} %get-tuple-element.23), channel_id=1, source_target_pairs={{1,0},{2,1},{3,2},{4,3},{5,4},{6,5},{7,6},{8,7},{9,8},{10,9},{11,1... | collective-permute-start | bytes 1130504 | tf_op jit(solution)/shard_map/ppermute | solution.py:412
  35.3 21.3 %all-to-all-done.1.fields_ref = f32[16,6,2,16,128]{4,3,2,1,0:T(8,128)S(1)} async-done(((f32[16,6,2,16,128]{4,3,2,1,0:T(8,128)}), f32[16,6,2,16,128]{4,3,2,1,0:T(8,128)S(1)}, u32[]{:S(2)}, u32[]{:S(2)}) %all-to-all-start.1) | async-done | bytes 1572896 | tf_op jit(solution)/shard_map/all_to_all | solution.py:416
  56.6 1.2 copy-done
  57.8 2.1 %shard_map.82 = (f32[96,128]{1,0:T(8,128)}, f32[96,128]{1,0:T(8,128)}) custom-call(f32[16,6,2,16,128]{4,3,2,1,0:T(8,128)} %copy-done), custom_call_target="tpu_custom_call" | custom-call | flops 2000000 | bytes 2000000 | tf_op jit(solution)/shard_map/pallas_call | solution.py:22
  59.9 5.7 %collective-permute-start.5 = (f32[96,128]{1,0:T(8,128)}, f32[96,128]{1,0:T(8,128)S(1)}, u32[]{:S(2)}, u32[]{:S(2)}) collective-permute-start(f32[96,128]{1,0:T(8,128)} %get-tuple-element.31), channel_id=1, source_target_pairs={{1,0},{2,1},{3,2},{4,3},{5,4},{6,5},{7,6},{8,7},{9,8},{10,9},{11,1... | collective-permute-start | bytes 147464 | tf_op jit(solution)/shard_map/ppermute | solution.py:412
  65.6 0.7 copy-done.4
  66.3 0.7 copy-done.5
  67.1 4.1 %shard_map.80 = (f32[16,16,128]{2,1,0:T(8,128)}, f32[16,16,128]{2,1,0:T(8,128)}, f32[16,256]{1,0:T(8,128)}) custom-call(s32[2]{0:T(128)} %pad_add_fusion.pq_ref, f32[32,16,256]{2,1,0:T(8,128)} %bitcast.4, f32[368,256]{1,0:T(8,128)} %copy-done.4, f32[368,256]{1,0:T(8,128)} %copy-done.5, f32[16,256]{1,0:T(8,128)} %get-tuple-element.21.base_ref.own_ref), custom_call_target="tpu_custom_call" | custom-call | flops 2000000 | bytes 2000000 | tf_op jit(solution)/shard_map/pallas_call | solution.py:22
  71.2 1.5 %collective-permute-start.3 = (f32[16,256]{1,0:T(8,128)}, f32[16,256]{1,0:T(8,128)S(1)}, u32[]{:S(2)}, u32[]{:S(2)}) collective-permute-start(f32[16,256]{1,0:T(8,128)} %get-tuple-element.26.own_ref), channel_id=1, source_target_pairs={{1,0},{2,1},{3,2},{4,3},{5,4},{6,5},{7,6},{8,7},{9,8},{10,9},{11,1... | collective-permute-start | bytes 49160 | tf_op jit(solution)/shard_map/ppermute | solution.py:412
  72.7 0.6 reshape.11.blocks_ref
  73.3 2.1 %shard_map.83.mat_ref = bf16[4,288,256]{2,1,0:T(8,128)(2,1)} custom-call(s32[27]{0:T(128)} %pattern_ref.1, f32[72]{0:T(128)} %reshape.11.blocks_ref), custom_call_target="tpu_custom_call" | custom-call | flops 2000000 | bytes 2000000 | tf_op jit(solution)/shard_map/pallas_call | solution.py:22
  75.4 2.1 %collective-permute-done.2.refs_0_ = f32[16,256]{1,0:T(8,128)S(1)} collective-permute-done((f32[16,256]{1,0:T(8,128)}, f32[16,256]{1,0:T(8,128)S(1)}, u32[]{:S(2)}, u32[]{:S(2)}) %collective-permute-start.2) | collective-permute-done | bytes 16416 | tf_op jit(solution)/shard_map/ppermute | solution.py:412
  78.1 4.1 %shard_map.81 = (f32[16,16,128]{2,1,0:T(8,128)}, f32[16,16,128]{2,1,0:T(8,128)}, f32[16,256]{1,0:T(8,128)}) custom-call(s32[2]{0:T(128)} %pad_add_fusion.pq_ref, f32[32,16,256]{2,1,0:T(8,128)} %bitcast.5, f32[368,256]{1,0:T(8,128)} %copy-done.4, f32[368,256]{1,0:T(8,128)} %copy-done.5, f32[16,256]{1,0:T(8,128)} %get-tuple-element.26.own_ref, ...), custom_call_target="tpu_custom_call" | custom-call | flops 2000000 | bytes 2000000 | tf_op jit(solution)/shard_map/pallas_call | solution.py:22
  83.5 5.2 %shard_map.84.d0_ref = f32[32,16,128]{2,1,0:T(8,128)} custom-call(s32[2]{0:T(128)} %pad_add_fusion.pq_ref, f32[16,6,2,16,128]{4,3,2,1,0:T(8,128)} %copy-done, f32[96,128]{1,0:T(8,128)} %copy-done.6, f32[96,128]{1,0:T(8,128)} %copy-done.7, bf16[4,288,256]{2,1,0:T(8,128)(2,1)} %shard_map.83.mat_ref), custom_call_target="tpu_custom_call" | custom-call | flops 2000000 | bytes 2000000 | tf_op jit(solution)/shard_map/pallas_call | solution.py:22
  88.7 3.5 %shard_map.85 = (f32[32,16,128]{2,1,0:T(8,128)}, f32[32,16,128]{2,1,0:T(8,128)}, f32[32,16,128]{2,1,0:T(8,128)}, f32[32,16,128]{2,1,0:T(8,128)}, f32[800,128]{1,0:T(8,128)}, /*index=5*/f32[800,128]{1,0:T(8,128)}) custom-call(s32[2]{0:T(128)} %pad_add_fusion.pq_ref, f32[16,16,128]{2,1,0:T(8,128)} %get-tuple-element.24.p0_ref, ...), custom_call_target="tpu_custom_call" | custom-call | flops 2000000 | bytes 2000000 | tf_op jit(solution)/shard_map/pallas_call | solution.py:22
  92.1 3.6 %collective-permute-start.7 = (f32[800,128]{1,0:T(8,128)}, f32[800,128]{1,0:T(8,128)S(1)}, u32[]{:S(2)}, u32[]{:S(2)}) collective-permute-start(f32[800,128]{1,0:T(8,128)} %get-tuple-element.37), channel_id=1, source_target_pairs={{1,0},{2,1},{3,2},{4,3},{5,4},{6,5},{7,6},{8,7},{9,8},{10,9},{11,1... | collective-permute-start | bytes 1228808 | tf_op jit(solution)/shard_map/ppermute | solution.py:412
  95.7 7.9 %collective-permute-done.6.upper_ref = f32[800,128]{1,0:T(8,128)S(1)} collective-permute-done((f32[800,128]{1,0:T(8,128)}, f32[800,128]{1,0:T(8,128)S(1)}, u32[]{:S(2)}, u32[]{:S(2)}) %collective-permute-start.6) | collective-permute-done | bytes 409632 | tf_op jit(solution)/shard_map/ppermute | solution.py:412
  103.6 0.8 copy-done.2
  104.5 3.2 %shard_map.86 = (f32[8,16,128]{2,1,0:T(8,128)}, f32[16,128]{1,0:T(8,128)}) custom-call(s32[2]{0:T(128)} %pad_add_fusion.pq_ref, f32[32,16,128]{2,1,0:T(8,128)} %get-tuple-element.32.a_ref, f32[32,16,128]{2,1,0:T(8,128)} %get-tuple-element.33.b_ref, f32[32,16,128]{2,1,0:T(8,128)} %get-tuple-element.34.e_ref, f32[32,16,128]{2,1,0:T(8,128)} %get-tuple-element.35.f_ref, ...), custom_call_target="tpu_custom_call" | custom-call | flops 2000000 | bytes 2000000 | tf_op jit(solution)/shard_map/pallas_call | solution.py:22
  107.7 3.1 %collective-permute-start.9 = (f32[16,128]{1,0:T(8,128)}, f32[16,128]{1,0:T(8,128)S(1)}, u32[]{:S(2)}, u32[]{:S(2)}) collective-permute-start(f32[16,128]{1,0:T(8,128)} %get-tuple-element.38.refs_0_), channel_id=1, source_target_pairs={{1,0},{2,1},{3,2},{4,3},{5,4},{6,5},{7,6},{8,7},{9,8},{10,9},{11,1... | collective-permute-start | bytes 24584 | tf_op jit(solution)/shard_map/ppermute | solution.py:412
  110.9 6.1 %shard_map.87.refs_4_ = f32[16,3,16,128]{3,2,1,0:T(8,128)} custom-call(s32[2]{0:T(128)} %pad_add_fusion.pq_ref, f32[16,16,128]{2,1,0:T(8,128)} %get-tuple-element.24.p0_ref, f32[16,16,128]{2,1,0:T(8,128)} %get-tuple-element.27.p1_ref, f32[16,6,2,16,128]{4,3,2,1,0:T(8,128)} %copy-done, f32[800,128]{1,0:T(8,128)} %copy-done.2, f32[800,128]{1,0:T(8,128)} %copy-done.3, ...), custom_call_target="tpu_custom_call" | custom-call | flops 2000000 | bytes 2000000 | tf_op jit(solution)/shard_map/pallas_call | solution.py:22
  117.6 3.6 %shard_map.88 = f32[16,4,16,128]{3,2,1,0:T(8,128)} custom-call(s32[2]{0:T(128)} %pad_add_fusion.pq_ref, f32[32,16,128]{2,1,0:T(8,128)} %get-tuple-element.32.a_ref, f32[32,16,128]{2,1,0:T(8,128)} %get-tuple-element.33.b_ref, f32[32,16,128]{2,1,0:T(8,128)} %get-tuple-element.34.e_ref, f32[32,16,128]{2,1,0:T(8,128)} %get-tuple-element.35.f_ref, ...), custom_call_target="tpu_custom_call" | custom-call | flops 2000000 | bytes 2000000 | tf_op jit(solution)/shard_map/pallas_call | solution.py:22
  121.2 19.7 %all_to_all.15.in_ref = f32[16,4,16,128]{3,2,1,0:T(8,128)} all-to-all(f32[16,4,16,128]{3,2,1,0:T(8,128)} %shard_map.88), channel_id=1, replica_groups=mesh['build'=16,'lat'=16] {'build'}, dimensions={0} | all-to-all | bytes 1048576 | tf_op jit(solution)/shard_map/all_to_all | solution.py:416
  140.9 2.0 %shard_map.89 = (f32[3,2,16,1024]{3,2,1,0:T(8,128)}, f32[2,16,1024]{2,1,0:T(8,128)}) custom-call(f32[16,4,16,128]{3,2,1,0:T(8,128)} %all_to_all.15.in_ref), custom_call_target="tpu_custom_call" | custom-call | flops 2000000 | bytes 2000000 | tf_op jit(solution)/shard_map/pallas_call | solution.py:22
  (35 shorter events, 3.2 us)
Async XLA Ops:
  2.5 19.6 %all-to-all-start = ((f32[16,2,16,256]{3,2,1,0:T(8,128)}), f32[16,2,16,256]{3,2,1,0:T(8,128)S(1)}, u32[]{:S(2)}, u32[]{:S(2)}) async-start(f32[16,2,16,256]{3,2,1,0:T(8,128)} %shard_map.77), calls=%async_computation | async-start | bytes 1048576 | tf_op jit(solution)/shard_map/all_to_all | solution.py:416
  22.1 0.8 copy-start.1
  22.9 33.7 %all-to-all-start.1 = ((f32[16,6,2,16,128]{4,3,2,1,0:T(8,128)}), f32[16,6,2,16,128]{4,3,2,1,0:T(8,128)S(1)}, u32[]{:S(2)}, u32[]{:S(2)}) async-start(f32[16,6,2,16,128]{4,3,2,1,0:T(8,128)} %get-tuple-element.29), calls=%async_computation.1 | async-start | bytes 3145728 | tf_op jit(solution)/shard_map/all_to_all | solution.py:416
  29.6 43.0 %copy-start.12 = (f32[8,3,3]{0,2,1:T(4,128)S(1)}, f32[8,3,3]{0,2,1:T(4,128)}, u32[]{:S(2)}) copy-start(f32[8,3,3]{0,2,1:T(4,128)} %param.9) | copy-start | bytes 868
  29.6 36.0 %collective-permute-start = (f32[368,256]{1,0:T(8,128)}, f32[368,256]{1,0:T(8,128)S(1)}, u32[]{:S(2)}, u32[]{:S(2)}) collective-permute-start(f32[368,256]{1,0:T(8,128)} %get-tuple-element.22), channel_id=1, source_target_pairs={{0,1},{1,2},{2,3},{3,4},{4,5},{5,6},{6,7},{7,8},{8,9},{9,10},{10,1... | collective-permute-start | bytes 1130504 | tf_op jit(solution)/shard_map/ppermute | solution.py:412
  31.3 34.3 %collective-permute-start.1 = (f32[368,256]{1,0:T(8,128)}, f32[368,256]{1,0:T(8,128)S(1)}, u32[]{:S(2)}, u32[]{:S(2)}) collective-permute-start(f32[368,256]{1,0:T(8,128)} %get-tuple-element.23), channel_id=1, source_target_pairs={{1,0},{2,1},{3,2},{4,3},{5,4},{6,5},{7,6},{8,7},{9,8},{10,9},{11,1... | collective-permute-start | bytes 1130504 | tf_op jit(solution)/shard_map/ppermute | solution.py:412
  56.6 1.2 copy-start
  59.9 22.4 %collective-permute-start.4 = (f32[96,128]{1,0:T(8,128)}, f32[96,128]{1,0:T(8,128)S(1)}, u32[]{:S(2)}, u32[]{:S(2)}) collective-permute-start(f32[96,128]{1,0:T(8,128)} %get-tuple-element.30), channel_id=1, source_target_pairs={{0,1},{1,2},{2,3},{3,4},{4,5},{5,6},{6,7},{7,8},{8,9},{9,10},{10,1... | collective-permute-start | bytes 147464 | tf_op jit(solution)/shard_map/ppermute | solution.py:412
  59.9 22.4 %collective-permute-start.5 = (f32[96,128]{1,0:T(8,128)}, f32[96,128]{1,0:T(8,128)S(1)}, u32[]{:S(2)}, u32[]{:S(2)}) collective-permute-start(f32[96,128]{1,0:T(8,128)} %get-tuple-element.31), channel_id=1, source_target_pairs={{1,0},{2,1},{3,2},{4,3},{5,4},{6,5},{7,6},{8,7},{9,8},{10,9},{11,1... | collective-permute-start | bytes 147464 | tf_op jit(solution)/shard_map/ppermute | solution.py:412
  65.6 0.7 copy-start.4
  66.3 0.7 copy-start.5
  71.2 4.3 %collective-permute-start.3 = (f32[16,256]{1,0:T(8,128)}, f32[16,256]{1,0:T(8,128)S(1)}, u32[]{:S(2)}, u32[]{:S(2)}) collective-permute-start(f32[16,256]{1,0:T(8,128)} %get-tuple-element.26.own_ref), channel_id=1, source_target_pairs={{1,0},{2,1},{3,2},{4,3},{5,4},{6,5},{7,6},{8,7},{9,8},{10,9},{11,1... | collective-permute-start | bytes 49160 | tf_op jit(solution)/shard_map/ppermute | solution.py:412
  72.6 4.9 %collective-permute-start.2 = (f32[16,256]{1,0:T(8,128)}, f32[16,256]{1,0:T(8,128)S(1)}, u32[]{:S(2)}, u32[]{:S(2)}) collective-permute-start(f32[16,256]{1,0:T(8,128)} %get-tuple-element.26.own_ref), channel_id=1, source_target_pairs={{0,1},{1,2},{2,3},{3,4},{4,5},{5,6},{6,7},{7,8},{8,9},{9,10},{10,1... | collective-permute-start | bytes 49160 | tf_op jit(solution)/shard_map/ppermute | solution.py:412
  75.4 2.1 %copy-start.8 = (f32[16,256]{1,0:T(8,128)}, f32[16,256]{1,0:T(8,128)S(1)}, u32[]{:S(2)}) copy-start(f32[16,256]{1,0:T(8,128)S(1)} %collective-permute-done.3.refs_1_) | copy-start | bytes 49156
  77.5 0.6 copy-start.9
  82.3 0.6 copy-start.6
  82.9 0.6 copy-start.7
  92.1 11.4 %collective-permute-start.6 = (f32[800,128]{1,0:T(8,128)}, f32[800,128]{1,0:T(8,128)S(1)}, u32[]{:S(2)}, u32[]{:S(2)}) collective-permute-start(f32[800,128]{1,0:T(8,128)} %get-tuple-element.36), channel_id=1, source_target_pairs={{0,1},{1,2},{2,3},{3,4},{4,5},{5,6},{6,7},{7,8},{8,9},{9,10},{10,1... | collective-permute-start | bytes 1228808 | tf_op jit(solution)/shard_map/ppermute | solution.py:412
  92.1 11.4 %collective-permute-start.7 = (f32[800,128]{1,0:T(8,128)}, f32[800,128]{1,0:T(8,128)S(1)}, u32[]{:S(2)}, u32[]{:S(2)}) collective-permute-start(f32[800,128]{1,0:T(8,128)} %get-tuple-element.37), channel_id=1, source_target_pairs={{1,0},{2,1},{3,2},{4,3},{5,4},{6,5},{7,6},{8,7},{9,8},{10,9},{11,1... | collective-permute-start | bytes 1228808 | tf_op jit(solution)/shard_map/ppermute | solution.py:412
  103.6 0.8 copy-start.2
  103.6 0.9 copy-start.3
  107.7 9.3 %collective-permute-start.9 = (f32[16,128]{1,0:T(8,128)}, f32[16,128]{1,0:T(8,128)S(1)}, u32[]{:S(2)}, u32[]{:S(2)}) collective-permute-start(f32[16,128]{1,0:T(8,128)} %get-tuple-element.38.refs_0_), channel_id=1, source_target_pairs={{1,0},{2,1},{3,2},{4,3},{5,4},{6,5},{7,6},{8,7},{9,8},{10,9},{11,1... | collective-permute-start | bytes 24584 | tf_op jit(solution)/shard_map/ppermute | solution.py:412
  110.9 6.1 %collective-permute-start.8 = (f32[16,128]{1,0:T(8,128)}, f32[16,128]{1,0:T(8,128)S(1)}, u32[]{:S(2)}, u32[]{:S(2)}) collective-permute-start(f32[16,128]{1,0:T(8,128)} %get-tuple-element.38.refs_0_), channel_id=1, source_target_pairs={{0,1},{1,2},{2,3},{3,4},{4,5},{5,6},{6,7},{7,8},{8,9},{9,10},{10,1... | collective-permute-start | bytes 24584 | tf_op jit(solution)/shard_map/ppermute | solution.py:412
  117.0 0.6 copy-start.10
  117.0 0.6 copy-start.11

commit v2 on v1

--- a/solution.py
+++ b/solution.py
@@ -6,6 +6,7 @@
 from jax.experimental import pallas as pl
 from jax.experimental.pallas import tpu as pltpu
 from jax.sharding import PartitionSpec as P
+
 
 smooth_eps = 0.0001
 root_eps = 0.01
@@ -17,15 +18,25 @@
 SM = pl.BlockSpec(memory_space=pltpu.SMEM)
 
 
-def call(kernel, outs, args, scratch=(), smem=0, cost=2000000):
+def call(kernel, outs, args, scratch=(), smem=0, micros=1.0, room=6):
     specs = [SM] * smem + [VM] * (len(args) - smem)
+    name = getattr(kernel, "func", kernel).__name__
+    if isinstance(kernel, functools.partial):
+        name += str(kernel.args[0])
+    return run(kernel, outs, args, specs, scratch, micros, room)
+
+
+def run(kernel, outs, args, specs, scratch, micros, room):
     return pl.pallas_call(
         kernel,
         out_shape=[jax.ShapeDtypeStruct(s, d) for s, d in outs],
         in_specs=specs,
         out_specs=[VM] * len(outs),
         scratch_shapes=list(scratch),
-        cost_estimate=pl.CostEstimate(flops=cost, bytes_accessed=cost, transcendentals=0),
+        compiler_params=pltpu.CompilerParams(vmem_limit_bytes=room << 20),
+        cost_estimate=pl.CostEstimate(
+            flops=0, bytes_accessed=int(micros * 3690000), transcendentals=0
+        ),
     )(*args)
 
 
@@ -65,20 +76,36 @@
         out_ref[p, :, :, 128:256] = second.reshape(2, 16, 128)
 
 
-def prepare_fields(pq_ref, disp_ref, adj_ref, mask_ref, out_ref, base_ref, wide_ref):
+def pack_edges(disp_ref, adj_ref, up_ref, down_ref):
     for number, ref in ((0, disp_ref), (3, adj_ref)):
         for c in range(3):
-            s = shifted_tiles(ref[c].reshape(32, 1024))
-            w = [pltpu.roll(t, 64, 1) for t in s]
-            low = lane(s[0].shape) < 64
-            for p in range(16):
-                k = p // 2 + 1
-                first = s[k] if p % 2 == 0 else jnp.where(low, w[k], w[k + 1])
-                out_ref[p, number + c] = first.reshape(2, 16, 128)
+            for i in range(2):
+                start = (number + c) * 2 + i
+                up_ref[start : start + 1] = ref[c, i, 0:1]
+                down_ref[start : start + 1] = ref[c, i, 15:16]
+
+
+def prepare_fields(disp_ref, adj_ref, mask_ref, upper_ref, lower_ref, out_ref, base_ref, wide_ref):
+    def tiles_of(x):
+        s = shifted_tiles(x)
+        w = [pltpu.roll(t, 64, 1) for t in s]
+        low = lane(s[0].shape) < 64
+        for p in range(16):
+            k = p // 2 + 1
+            yield p, s[k] if p % 2 == 0 else jnp.where(low, w[k], w[k + 1])
+
+    for number, ref in ((0, disp_ref), (3, adj_ref)):
+        for c in range(3):
+            start = (number + c) * 32
+            for p, tile in tiles_of(ref[c].reshape(32, 1024)):
+                out_ref[p, start : start + 32] = tile
+    for h, (ref, keep) in enumerate(zip((upper_ref, lower_ref), edges_of())):
+        for p, tile in tiles_of(ref[...] * keep):
+            out_ref[p, pl.ds(192 + h, 12, stride=2)] = tile[0:12]
     base = base_floor + (1.0 - base_floor) * mask_ref[...].astype(f32)
     for t, tile in enumerate(shifted_tiles(base)):
         wide_ref[:, 128 * t : 128 * t + 128] = tile
-    p = pq_ref[0]
+    p = lax.axis_index("build")
     k = lax.div(p, 2)
     odd = (p - 2 * k).astype(f32)
     before, here, after = [wide_ref[:, pl.ds(pl.multiple_of((k + t) * 128, 128), 128)] for t in range(3)]
@@ -107,9 +134,11 @@
                     for da in (-1, 0, 1):
                         sign = -1 if kind == 0 else 1
                         o = 9 * (sign * da + 1) + 3 * (sign * db + 1) + (sign * ds + 1)
-                        start = pattern_ref[o] * 9
+                        start = pattern_ref[o]
                         for d in range(3):
-                            values[da, d] = blocks_ref[start + (d * 3 + c if kind == 0 else c * 3 + d)]
+                            values[da, d] = (
+                                blocks_ref[start, d, c] if kind == 0 else blocks_ref[start, c, d]
+                            )
                     for zi in range(2):
                         r = jnp.zeros((8, 256), f32)
                         for da in (-1, 0, 1):
@@ -128,18 +157,18 @@
                     out_ref[2 * kind + 1, start : start + 16] = low
 
 
-def pack_density(dens_ref, base_ref, up_ref, down_ref):
-    up_ref[0:16] = base_ref[...]
-    down_ref[0:16] = base_ref[...]
-    for ph in range(2):
+def pack_density(dens_ref, base_ref, up0_ref, down0_ref, up1_ref, down1_ref):
+    up0_ref[176:192] = base_ref[...]
+    down0_ref[176:192] = base_ref[...]
+    for ph, up_ref, down_ref in ((0, up0_ref, down0_ref), (1, up1_ref, down1_ref)):
         for j in range(15):
             x = dens_ref[16 * ph + j]
             if j < 7:
-                start = 16 + ph * 176 + j * 16
+                start = j * 16
                 up_ref[start : start + 16] = x
                 down_ref[start : start + 16] = x
             else:
-                start = 16 + ph * 176 + 112 + (j - 7) * 8
+                start = 112 + (j - 7) * 8
                 up_ref[start : start + 8] = x[0:8]
                 down_ref[start : start + 8] = x[8:16]
 
@@ -155,14 +184,14 @@
     )
 
 
-def forward(ph, pq_ref, dens_ref, upper_ref, lower_ref, own_ref, *refs):
+def forward(ph, dens_ref, upper_ref, lower_ref, own_ref, *refs):
     if ph == 0:
-        up, down = upper_ref[0:16], lower_ref[0:16]
-        printed_ref, support_ref, state_ref = refs
+        up, down = upper_ref[176:192], lower_ref[176:192]
+        printed_ref, gain_ref, kept_ref, state_ref = refs
     else:
-        su_ref, sd_ref, printed_ref, support_ref, state_ref = refs
+        su_ref, sd_ref, printed_ref, gain_ref, kept_ref, state_ref = refs
         up, down = su_ref[...], sd_ref[...]
-    p, q = pq_ref[0], pq_ref[1]
+    p, q = lax.axis_index("build"), lax.axis_index("lat")
     current = jnp.concatenate([up, own_ref[...], down], 0)
     l = lane((48, 256))
     y = 64 * p - 32 + l - jnp.where(l < 192, 0, 256)
@@ -182,32 +211,29 @@
         design = dens_ref[16 * ph + j]
         if j < 15:
             size = 16 if j < 7 else 8
-            start = 16 + ph * 176 + (j * 16 if j < 7 else 112 + (j - 7) * 8)
+            start = j * 16 if j < 7 else 112 + (j - 7) * 8
             design = jnp.concatenate(
                 [upper_ref[start : start + size], design, lower_ref[start : start + size]], 0
             )
-        support = jnp.sqrt(jnp.sqrt(jnp.sqrt(jnp.sqrt(cross))))
+        support = lax.rsqrt(lax.rsqrt(lax.rsqrt(lax.rsqrt(cross))))
         differ = design - support
-        current = 0.5 * (design + support - jnp.sqrt(differ * differ + smooth_eps) + root_eps)
+        square = differ * differ + smooth_eps
+        inverse = lax.rsqrt(square)
+        current = 0.5 * (design + support - square * inverse + root_eps)
         edge = (rows - 16) // 2
         printed_ref[j] = current[edge : edge + 16, 0:128]
-        support_ref[j] = support[edge : edge + 16, 0:128]
+        slope = (differ * inverse)[edge : edge + 16, 0:128]
+        s1 = support[edge : edge + 16, 0:128]
+        s3 = s1 * s1 * s1
+        s6 = s3 * s3
+        gain_ref[j] = 0.5 * (1.0 + slope) / (s6 * s6 * s3)
+        kept_ref[j] = 0.5 * (1.0 - slope)
     state_ref[...] = current
 
 
-def pack_rows(fields_ref, up_ref, down_ref):
-    for c in range(3):
-        for z in range(32):
-            x = fields_ref[z // 2, 3 + c, z % 2]
-            up_ref[c * 32 + z : c * 32 + z + 1] = x[0:1]
-            down_ref[c * 32 + z : c * 32 + z + 1] = x[15:16]
-
-
-def fill_halo(halo, upper, lower):
-    halo[...] = jnp.zeros(halo.shape, f32)
-    for c in range(3):
-        halo[c, pl.ds(2, 32, stride=2)] = upper[c * 32 : c * 32 + 32]
-        halo[c, pl.ds(3, 32, stride=2)] = lower[c * 32 : c * 32 + 32]
+def layer_of(fields_ref, c, z):
+    start = (c * 2 + z % 2) * 16
+    return fields_ref[z // 2, start : start + 16]
 
 
 def product(field, halo, mat_ref, kind, i):
@@ -234,56 +260,53 @@
     return pick
 
 
-def edges_of(pq_ref):
-    q = pq_ref[1]
+def edges_of():
+    q = lax.axis_index("lat")
     return jnp.where(q > 0, 1.0, 0.0), jnp.where(q < 15, 1.0, 0.0)
 
 
-def direct_part(pq_ref, fields_ref, upper_ref, lower_ref, mat_ref, out_ref, field, halo):
-    keep_up, keep_down = edges_of(pq_ref)
-    fill_halo(halo, upper_ref[...] * keep_up, lower_ref[...] * keep_down)
+def direct_part(fields_ref, mat_ref, out_ref, field, halo):
+    halo[...] = jnp.zeros(halo.shape, f32)
     for c in range(3):
         field[c, 0] = jnp.zeros((16, 128), f32)
         field[c, 33] = jnp.zeros((16, 128), f32)
         for z in range(32):
-            field[c, z + 1] = fields_ref[z // 2, 3 + c, z % 2]
+            field[c, z + 1] = layer_of(fields_ref, 3 + c, z)
+        for k in range(16):
+            start = 192 + (3 + c) * 4
+            halo[c, 4 * k + 2 : 4 * k + 6] = fields_ref[k, start : start + 4]
 
     def body(i, carry):
         pick = product(field, halo, mat_ref, 0, i)
         for pair in range(2):
             for zi in range(2):
-                total = fields_ref[2 * i + pair, 0, zi] * pick(pair, 0, zi)
+                total = fields_ref[2 * i + pair, zi * 16 : zi * 16 + 16] * pick(pair, 0, zi)
                 for c in (1, 2):
-                    total = total + fields_ref[2 * i + pair, c, zi] * pick(pair, c, zi)
+                    start = (c * 2 + zi) * 16
+                    total = total + fields_ref[2 * i + pair, start : start + 16] * pick(pair, c, zi)
                 out_ref[4 * i + 2 * pair + zi] = total
         return carry
 
     lax.fori_loop(0, 8, body, 0)
 
 
-def coefficients(pq_ref, p0_ref, s0_ref, p1_ref, s1_ref, dens_ref, d0_ref, fields_ref, *refs):
-    a_ref, b_ref, e_ref, f_ref, up_ref, down_ref = refs
-    y = 64 * pq_ref[0] - 32 + lane((16, 128))
+def coefficients(p0_ref, g0_ref, k0_ref, p1_ref, g1_ref, k1_ref, d0_ref, *refs):
+    a_ref, b_ref, e_ref, f_ref = refs[:4]
+    y = 64 * lax.axis_index("build") - 32 + lane((16, 128))
     inside = (y >= 0) & (y < 1024)
     for z in range(32):
         ph, j = divmod(z, 16)
         printed = (p0_ref, p1_ref)[ph][j]
-        support = (s0_ref, s1_ref)[ph][j]
-        design = dens_ref[z, :, 0:128]
+        gain = (g0_ref, g1_ref)[ph][j]
+        kept = (k0_ref, k1_ref)[ph][j]
         p2 = printed * printed
         p3 = p2 * printed
-        modulus = modulus_floor + (1.0 - modulus_floor) * p3
         p6 = p3 * p3
         p15 = p6 * p6 * p3
-        s2 = support * support
-        s3 = s2 * support
-        s6 = s3 * s3
-        s15 = s6 * s6 * s3
-        differ = design - support
-        slope = differ / jnp.sqrt(differ * differ + smooth_eps)
         direct = d0_ref[z] * (3.0 * (1.0 - modulus_floor)) * p2
-        gain = 0.5 * (1.0 + slope) / s15
-        kept = 0.5 * (1.0 - slope)
+        modulus = modulus_floor + (1.0 - modulus_floor) * p3
+        refs[6][352 + z : 353 + z] = modulus[0:1]
+        refs[7][352 + z : 353 + z] = modulus[15:16]
         zero = jnp.zeros_like(direct)
         a = jnp.where(inside, direct * gain, zero)
         b = jnp.where(inside, p15 * gain, zero)
@@ -291,8 +314,9 @@
         b_ref[z] = b
         e_ref[z] = direct * kept
         f_ref[z] = p15 * kept
+        up_ref, down_ref = refs[4 + 2 * ph : 6 + 2 * ph]
         for number, value in ((0, a), (1, b)):
-            start = (number * 2 + ph) * 176
+            start = number * 176
             if 1 <= j <= 8:
                 start += (j - 1) * 8
                 up_ref[start : start + 8] = value[0:8]
@@ -301,24 +325,23 @@
                 start += 64 + (j - 9) * 16
                 up_ref[start : start + 16] = value
                 down_ref[start : start + 16] = value
-        for c in range(3):
-            u = modulus * fields_ref[z // 2, c, z % 2]
-            start = 704 + c * 32 + z
-            up_ref[start : start + 1] = u[0:1]
-            down_ref[start : start + 1] = u[15:16]
-
-
-def force_part(pq_ref, p0_ref, p1_ref, fields_ref, upper_ref, lower_ref, mat_ref, out_ref, field, halo):
-    keep_up, keep_down = edges_of(pq_ref)
-    fill_halo(halo, upper_ref[704:800] * keep_up, lower_ref[704:800] * keep_down)
+
+
+def force_part(p0_ref, p1_ref, fields_ref, upper_ref, lower_ref, mat_ref, out_ref, field, halo, rim):
+    halo[...] = jnp.zeros(halo.shape, f32)
+    rim[pl.ds(2, 32, stride=2)] = upper_ref[352:384]
+    rim[pl.ds(3, 32, stride=2)] = lower_ref[352:384]
     for c in range(3):
         field[c, 0] = jnp.zeros((16, 128), f32)
         field[c, 33] = jnp.zeros((16, 128), f32)
+        for k in range(16):
+            start = 192 + c * 4
+            halo[c, 4 * k + 2 : 4 * k + 6] = fields_ref[k, start : start + 4] * rim[4 * k + 2 : 4 * k + 6]
     for z in range(32):
         printed = (p0_ref, p1_ref)[z // 16][z % 16]
         modulus = modulus_floor + (1.0 - modulus_floor) * (printed * printed * printed)
         for c in range(3):
-            field[c, z + 1] = modulus * fields_ref[z // 2, c, z % 2]
+            field[c, z + 1] = modulus * layer_of(fields_ref, c, z)
 
     def body(i, carry):
         pick = product(field, halo, mat_ref, 1, i)
@@ -333,8 +356,8 @@
     lax.fori_loop(0, 8, body, 0)
 
 
-def backward(ph, pq_ref, a_ref, b_ref, e_ref, f_ref, upper_ref, lower_ref, *refs):
-    keep_up, keep_down = edges_of(pq_ref)
+def backward(ph, a_ref, b_ref, e_ref, f_ref, upper_ref, lower_ref, *refs):
+    keep_up, keep_down = edges_of()
     if ph == 1:
         sens_ref, state_ref = refs
         current = None
@@ -353,7 +376,7 @@
             value = ref[z]
             if j >= 1:
                 size = 8 if j <= 8 else 16
-                start = (number * 2 + ph) * 176 + ((j - 1) * 8 if j <= 8 else 64 + (j - 9) * 16)
+                start = number * 176 + ((j - 1) * 8 if j <= 8 else 64 + (j - 9) * 16)
                 value = jnp.concatenate(
                     [
                         upper_ref[start : start + size] * keep_up,
@@ -417,71 +440,67 @@
 
 
 def on_device(density, support_mask, pattern, blocks, displacement, adjoint):
-    pq = jnp.stack([lax.axis_index("build"), lax.axis_index("lat")]).astype(jnp.int32)
     (windows,) = call(prepare_density, [((16, 2, 16, 256), f32)], [density])
     dens = exchange(windows).reshape(32, 16, 256)
+    up, down = call(pack_edges, [((16, 1024), f32)] * 2, [displacement, adjoint])
+    upper, lower = trade(down, up)
     fields, base = call(
         prepare_fields,
-        [((16, 6, 2, 16, 128), f32), ((16, 256), f32)],
-        [pq, displacement, adjoint, support_mask],
+        [((16, 216, 128), f32), ((16, 256), f32)],
+        [displacement, adjoint, support_mask, upper, lower],
         scratch=[pltpu.VMEM((16, 11 * 128), f32)],
-        smem=1,
-    )
-    (mats,) = call(matrices, [((4, 288, 256), bf16)], [pattern, blocks.reshape(72)], smem=2)
+    )
     fields = exchange(fields)
-    up_send, down_send = call(pack_density, [((368, 256), f32)] * 2, [dens, base])
-    upper, lower = trade(down_send, up_send)
+    up0, down0, up1, down1 = call(
+        pack_density, [((192, 256), f32)] * 2 + [((176, 256), f32)] * 2, [dens, base], micros=0.2
+    )
+    upper0, lower0 = trade(down0, up0)
+    upper1, lower1 = trade(down1, up1)
     layer = ((16, 16, 128), f32)
-    p0, s0, state = call(
+    p0, g0, k0, state = call(
         functools.partial(forward, 0),
-        [layer, layer, ((16, 256), f32)],
-        [pq, dens, upper, lower, base],
-        smem=1,
+        [layer] * 3 + [((16, 256), f32)],
+        [dens, upper0, lower0, base],
+        micros=2.0,
     )
     state_up, state_down = trade(state, state)
-    p1, s1, _ = call(
+    (mats,) = call(matrices, [((4, 288, 256), bf16)], [pattern, blocks], smem=2, micros=1.4)
+    p1, g1, k1, _ = call(
         functools.partial(forward, 1),
-        [layer, layer, ((16, 256), f32)],
-        [pq, dens, upper, lower, state, state_up, state_down],
-        smem=1,
-    )
-    up_send, down_send = call(pack_rows, [((96, 128), f32)] * 2, [fields])
-    adj_up, adj_down = trade(down_send, up_send)
+        [layer] * 3 + [((16, 256), f32)],
+        [dens, upper1, lower1, state, state_up, state_down],
+        micros=2.0,
+    )
     work = [pltpu.VMEM((3, 34, 16, 128), f32), pltpu.VMEM((3, 72, 128), f32)]
-    (d0,) = call(
-        direct_part,
-        [((32, 16, 128), f32)],
-        [pq, fields, adj_up, adj_down, mats],
-        scratch=work,
-        smem=1,
-    )
     whole = ((32, 16, 128), f32)
-    a, b, e, f, up_send, down_send = call(
+    (d0,) = call(direct_part, [whole], [fields, mats], scratch=work, micros=3.0)
+    rim = ((352, 128), f32)
+    rim_rows = ((384, 128), f32)
+    a, b, e, f, up0, down0, up1, down1 = call(
         coefficients,
-        [whole] * 4 + [((800, 128), f32)] * 2,
-        [pq, p0, s0, p1, s1, dens, d0, fields],
-        smem=1,
-    )
-    upper, lower = trade(down_send, up_send)
+        [whole] * 4 + [rim] * 2 + [rim_rows] * 2,
+        [p0, g0, k0, p1, g1, k1, d0],
+        micros=0.3,
+    )
+    upper1, lower1 = trade(down1, up1)
+    upper0, lower0 = trade(down0, up0)
+    (force,) = call(
+        force_part,
+        [((16, 3, 16, 128), f32)],
+        [p0, p1, fields, upper1, lower1, mats],
+        scratch=work + [pltpu.VMEM((72, 128), f32)],
+        micros=3.0,
+    )
     sens1, state = call(
         functools.partial(backward, 1),
         [((8, 16, 128), f32), ((16, 128), f32)],
-        [pq, a, b, e, f, upper, lower],
-        smem=1,
+        [a, b, e, f, upper1, lower1],
     )
     state_up, state_down = trade(state, state)
-    (force,) = call(
-        force_part,
-        [((16, 3, 16, 128), f32)],
-        [pq, p0, p1, fields, upper, lower, mats],
-        scratch=work,
-        smem=1,
-    )
     (packed,) = call(
         functools.partial(backward, 0),
         [((16, 4, 16, 128), f32)],
-        [pq, a, b, e, f, upper, lower, state, state_up, state_down, sens1, force],
-        smem=1,
+        [a, b, e, f, upper0, lower0, state, state_up, state_down, sens1, force],
     )
     packed = exchange(packed)
     return tuple(call(unpack, [((3, 2, 16, 1024), f32), ((2, 16, 1024), f32)], [packed]))

time: 144 us -> 108 us (0.75)
  Pallas kernels: 43 us -> 19.2 us
  waiting for transfers between devices: 38.8 us -> 17.3 us
  starting transfers between devices: 32.7 us -> 41.8 us
  blocking collectives: 19.7 us -> 23.1 us
  local copies, waits for them, and re-layouts: 7.5 us -> 5.81 us
    all_to_all x2, waiting for transfers between devices: 28.8 us -> 4.84 us  [exchange(): return lax.all_to_all(x, 'build', 0, 0, tiled=True)]
    pallas_call x13, Pallas kernels: 43 us -> 19.2 us  [run(): pl.pallas_call(kernel, out_shape=[jax.ShapeDtypeStruct(s, d) for s, d in...]
    ppermute x5 -> x7, starting transfers between devices: 17.9 us -> 24.5 us  [trade(): lax.ppermute(to_upper, 'lat', down)]
    all_to_all x1, blocking collectives: 19.7 us -> 23.1 us  [exchange(): return lax.all_to_all(x, 'build', 0, 0, tiled=True)]
    ppermute x5 -> x7, waiting for transfers between devices: 9.99 us -> 12.4 us  [trade(): lax.ppermute(to_lower, 'lat', up)]
    all_to_all x2, starting transfers between devices: 13.2 us -> 15.5 us  [exchange(): return lax.all_to_all(x, 'build', 0, 0, tiled=True)]
    unnamed x27 -> x31, local copies, waits for them, and re-layouts: 6.87 us -> 5.81 us
  transfers between devices with their start and end apart: 12 -> 16, of which waited for: 4 -> 7; matrix products, arithmetic and copies ran while one was open for 1% -> 0% of each run, Pallas kernels for 17% -> 12%
where the time goes in v2:
time: 108 us
  starting transfers between devices  41.8 us (39%)
  blocking collectives  23.1 us (21%)
  Pallas kernels  19.2 us (18%)
  waiting for transfers between devices  17.3 us (16%)
  local copies, waits for them, and re-layouts  5.81 us (5%)
    ppermute x7, starting transfers between devices, trade(): lax.ppermute(to_upper, 'lat', down)  24.5 us
    all_to_all x1, blocking collectives, exchange(): return lax.all_to_all(x, 'build', 0, 0, tiled=True)  23.1 us
    pallas_call x13, Pallas kernels, run(): pl.pallas_call(kernel, out_shape=[jax.ShapeDtypeStruct(s, d) for s, d in...  19.2 us
    all_to_all x2, starting transfers between devices, exchange(): return lax.all_to_all(x, 'build', 0, 0, tiled=True)  15.5 us
    ppermute x7, waiting for transfers between devices, trade(): lax.ppermute(to_lower, 'lat', up)  12.4 us
    unnamed x31, local copies, waits for them, and re-layouts  5.81 us
    all_to_all x2, waiting for transfers between devices, exchange(): return lax.all_to_all(x, 'build', 0, 0, tiled=True)  4.84 us
  transfers between devices with their start and end apart: 16, of which 7 were waited for; matrix products, arithmetic and copies ran while one was open for 0% of the time, Pallas kernels for 12%

profile of v2, /device:TPU:1, one launch (start us, length us, event | category | flops | bytes accessed | tf_op | source)
XLA Modules:
  0.0 107.9 jit_solution(2480144011350166748)
XLA Ops:
  0.7 1.0 copy-done.3
  1.6 1.0 shard_map.77
  2.6 8.4 %all-to-all-start = ((f32[16,2,16,256]{3,2,1,0:T(8,128)}), f32[16,2,16,256]{3,2,1,0:T(8,128)S(1)}, u32[]{:S(2)}, u32[]{:S(2)}) async-start(f32[16,2,16,256]{3,2,1,0:T(8,128)} %shard_map.77), calls=%async_computation | async-start | bytes 1048576 | tf_op jit(solution)/shard_map/all_to_all | solution.py:439
  11.1 1.7 %collective-permute-start = (f32[16,1024]{1,0:T(8,128)S(1)}, f32[16,1024]{1,0:T(8,128)S(1)}, u32[]{:S(2)}, u32[]{:S(2)}) collective-permute-start(f32[16,1024]{1,0:T(8,128)S(1)} %get-tuple-element.27), channel_id=1, source_target_pairs={{0,1},{1,2},{2,3},{3,4},{4,5},{5,6},{6,7},{7,8},{8,9},{9,10},{10,1... | collective-permute-start | bytes 196616 | tf_op jit(solution)/shard_map/ppermute | solution.py:435
  12.8 4.1 %collective-permute-start.1 = (f32[16,1024]{1,0:T(8,128)S(1)}, f32[16,1024]{1,0:T(8,128)S(1)}, u32[]{:S(2)}, u32[]{:S(2)}) collective-permute-start(f32[16,1024]{1,0:T(8,128)S(1)} %get-tuple-element.28), channel_id=1, source_target_pairs={{1,0},{2,1},{3,2},{4,3},{5,4},{6,5},{7,6},{8,7},{9,8},{10,9},{11,1... | collective-permute-start | bytes 196616 | tf_op jit(solution)/shard_map/ppermute | solution.py:435
  17.0 3.0 %collective-permute-done.upper_ref = f32[16,1024]{1,0:T(8,128)S(1)} collective-permute-done((f32[16,1024]{1,0:T(8,128)S(1)}, f32[16,1024]{1,0:T(8,128)S(1)}, u32[]{:S(2)}, u32[]{:S(2)}) %collective-permute-start) | collective-permute-done | bytes 65568 | tf_op jit(solution)/shard_map/ppermute | solution.py:435
  20.0 1.0 shard_map.79
  21.0 1.2 %copy-done = f32[16,216,128]{2,1,0:T(8,128)} copy-done((f32[16,216,128]{2,1,0:T(8,128)}, f32[16,216,128]{2,1,0:T(8,128)S(1)}, u32[]{:S(2)}) %copy-start) | copy-done | bytes 1769496
  22.2 1.2 %all-to-all-done = f32[16,2,16,256]{3,2,1,0:T(8,128)S(1)} async-done(((f32[16,2,16,256]{3,2,1,0:T(8,128)}), f32[16,2,16,256]{3,2,1,0:T(8,128)S(1)}, u32[]{:S(2)}, u32[]{:S(2)}) %all-to-all-start) | async-done | bytes 524320 | tf_op jit(solution)/shard_map/all_to_all | solution.py:439
  23.4 7.1 %all-to-all-start.1 = ((f32[16,216,128]{2,1,0:T(8,128)}), f32[16,216,128]{2,1,0:T(8,128)S(1)}, u32[]{:S(2)}, u32[]{:S(2)}) async-start(f32[16,216,128]{2,1,0:T(8,128)} %copy-done), calls=%async_computation.1 | async-start | bytes 3538944 | tf_op jit(solution)/shard_map/all_to_all | solution.py:439
  30.4 0.8 shard_map.80
  31.2 3.7 %collective-permute-start.3 = (f32[192,256]{1,0:T(8,128)S(1)}, f32[192,256]{1,0:T(8,128)S(1)}, u32[]{:S(2)}, u32[]{:S(2)}) collective-permute-start(f32[192,256]{1,0:T(8,128)S(1)} %get-tuple-element.31), channel_id=1, source_target_pairs={{1,0},{2,1},{3,2},{4,3},{5,4},{6,5},{7,6},{8,7},{9,8},{10,9},{11,1... | collective-permute-start | bytes 589832 | tf_op jit(solution)/shard_map/ppermute | solution.py:435
  34.9 3.6 %collective-permute-start.5 = (f32[176,256]{1,0:T(8,128)}, f32[176,256]{1,0:T(8,128)S(1)}, u32[]{:S(2)}, u32[]{:S(2)}) collective-permute-start(f32[176,256]{1,0:T(8,128)} %get-tuple-element.36), channel_id=1, source_target_pairs={{1,0},{2,1},{3,2},{4,3},{5,4},{6,5},{7,6},{8,7},{9,8},{10,9},{11,1... | collective-permute-start | bytes 540680 | tf_op jit(solution)/shard_map/ppermute | solution.py:435
  38.5 4.4 %collective-permute-done.2.upper_ref = f32[192,256]{1,0:T(8,128)S(1)} collective-permute-done((f32[192,256]{1,0:T(8,128)S(1)}, f32[192,256]{1,0:T(8,128)S(1)}, u32[]{:S(2)}, u32[]{:S(2)}) %collective-permute-start.2) | collective-permute-done | bytes 196640 | tf_op jit(solution)/shard_map/ppermute | solution.py:435
  42.9 1.9 %shard_map.81 = (f32[16,16,128]{2,1,0:T(8,128)S(1)}, f32[16,16,128]{2,1,0:T(8,128)S(1)}, f32[16,16,128]{2,1,0:T(8,128)S(1)}, f32[16,256]{1,0:T(8,128)S(1)}) custom-call(f32[32,16,256]{2,1,0:T(8,128)S(1)} %bitcast.2, f32[192,256]{1,0:T(8,128)S(1)} %collective-permute-done.2.upper_ref, f32[192,256]{1,0:T(8,128)S(1)} %collective-permute-done.3.lower_ref, ...), custom_call_target="tpu_custom_call" | custom-call | bytes 7380000 | tf_op jit(solution)/shard_map/pallas_call | solution.py:30
  45.4 2.1 %collective-permute-start.7 = (f32[16,256]{1,0:T(8,128)S(1)}, f32[16,256]{1,0:T(8,128)S(1)}, u32[]{:S(2)}, u32[]{:S(2)}) collective-permute-start(f32[16,256]{1,0:T(8,128)S(1)} %get-tuple-element.37.own_ref), channel_id=1, source_target_pairs={{1,0},{2,1},{3,2},{4,3},{5,4},{6,5},{7,6},{8,7},{9,8},{10,9},{11,1... | collective-permute-start | bytes 49160 | tf_op jit(solution)/shard_map/ppermute | solution.py:435
  48.3 1.4 %shard_map.83.mat_ref = bf16[4,288,256]{2,1,0:T(8,128)(2,1)S(1)} custom-call(s32[27]{0:T(128)S(1)} %copy-done.13, f32[8,3,3]{2,1,0:T(4,128)S(1)} %copy.8.blocks_ref), custom_call_target="tpu_custom_call" | custom-call | bytes 5166000 | tf_op jit(solution)/shard_map/pallas_call | solution.py:30
  49.7 2.8 %collective-permute-done.4.upper_ref = f32[176,256]{1,0:T(8,128)S(1)} collective-permute-done((f32[176,256]{1,0:T(8,128)}, f32[176,256]{1,0:T(8,128)S(1)}, u32[]{:S(2)}, u32[]{:S(2)}) %collective-permute-start.4) | collective-permute-done | bytes 180256 | tf_op jit(solution)/shard_map/ppermute | solution.py:435
  52.5 1.1 %collective-permute-done.6.refs_0_ = f32[16,256]{1,0:T(8,128)} collective-permute-done((f32[16,256]{1,0:T(8,128)S(1)}, f32[16,256]{1,0:T(8,128)}, u32[]{:S(2)}, u32[]{:S(2)}) %collective-permute-start.6) | collective-permute-done | bytes 16416 | tf_op jit(solution)/shard_map/ppermute | solution.py:435
  53.6 3.2 %shard_map.82 = (f32[16,16,128]{2,1,0:T(8,128)S(1)}, f32[16,16,128]{2,1,0:T(8,128)S(1)}, f32[16,16,128]{2,1,0:T(8,128)S(1)}, f32[16,256]{1,0:T(8,128)}) custom-call(f32[32,16,256]{2,1,0:T(8,128)S(1)} %bitcast.3, f32[176,256]{1,0:T(8,128)S(1)} %collective-permute-done.4.upper_ref, f32[176,256]{1,0:T(8,128)S(1)} %collective-permute-done.5.lower_ref, ...), custom_call_target="tpu_custom_call" | custom-call | bytes 7380000 | tf_op jit(solution)/shard_map/pallas_call | solution.py:30
  58.2 3.7 %all-to-all-done.1.fields_ref = f32[16,216,128]{2,1,0:T(8,128)S(1)} async-done(((f32[16,216,128]{2,1,0:T(8,128)}), f32[16,216,128]{2,1,0:T(8,128)S(1)}, u32[]{:S(2)}, u32[]{:S(2)}) %all-to-all-start.1) | async-done | bytes 1769504 | tf_op jit(solution)/shard_map/all_to_all | solution.py:439
  61.8 2.9 %shard_map.84.d0_ref = f32[32,16,128]{2,1,0:T(8,128)S(1)} custom-call(f32[16,216,128]{2,1,0:T(8,128)S(1)} %all-to-all-done.1.fields_ref, bf16[4,288,256]{2,1,0:T(8,128)(2,1)S(1)} %shard_map.83.mat_ref), custom_call_target="tpu_custom_call" | custom-call | bytes 11070000 | tf_op jit(solution)/shard_map/pallas_call | solution.py:30
  64.8 0.9 copy-done.7
  65.9 3.9 %collective-permute-start.11 = (f32[384,128]{1,0:T(8,128)S(1)}, f32[384,128]{1,0:T(8,128)S(1)}, u32[]{:S(2)}, u32[]{:S(2)}) collective-permute-start(f32[384,128]{1,0:T(8,128)S(1)} %get-tuple-element.49), channel_id=1, source_target_pairs={{1,0},{2,1},{3,2},{4,3},{5,4},{6,5},{7,6},{8,7},{9,8},{10,9},{11,1... | collective-permute-start | bytes 589832 | tf_op jit(solution)/shard_map/ppermute | solution.py:435
  69.9 3.6 %collective-permute-start.9 = (f32[352,128]{1,0:T(8,128)S(1)}, f32[352,128]{1,0:T(8,128)S(1)}, u32[]{:S(2)}, u32[]{:S(2)}) collective-permute-start(f32[352,128]{1,0:T(8,128)S(1)} %get-tuple-element.47), channel_id=1, source_target_pairs={{1,0},{2,1},{3,2},{4,3},{5,4},{6,5},{7,6},{8,7},{9,8},{10,9},{11,1... | collective-permute-start | bytes 540680 | tf_op jit(solution)/shard_map/ppermute | solution.py:435
  73.4 1.2 %shard_map.86 = (f32[8,16,128]{2,1,0:T(8,128)S(1)}, f32[16,128]{1,0:T(8,128)S(1)}) custom-call(f32[32,16,128]{2,1,0:T(8,128)S(1)} %get-tuple-element.42.a_ref, f32[32,16,128]{2,1,0:T(8,128)S(1)} %get-tuple-element.43.b_ref, f32[32,16,128]{2,1,0:T(8,128)S(1)} %get-tuple-element.44.e_ref, f32[32,16,128]{2,1,0:T(8,128)S(1)} %get-tuple-element.45.f_ref, ...), custom_call_target="tpu_custom_call" | custom-call | bytes 3690000 | tf_op jit(solution)/shard_map/pallas_call | solution.py:30
  74.6 3.5 %collective-permute-start.13 = (f32[16,128]{1,0:T(8,128)S(1)}, f32[16,128]{1,0:T(8,128)S(1)}, u32[]{:S(2)}, u32[]{:S(2)}) collective-permute-start(f32[16,128]{1,0:T(8,128)S(1)} %get-tuple-element.50.refs_0_), channel_id=1, source_target_pairs={{1,0},{2,1},{3,2},{4,3},{5,4},{6,5},{7,6},{8,7},{9,8},{10,9},{11,1... | collective-permute-start | bytes 24584 | tf_op jit(solution)/shard_map/ppermute | solution.py:435
  78.0 3.5 %shard_map.87.refs_4_ = f32[16,3,16,128]{3,2,1,0:T(8,128)S(1)} custom-call(f32[16,16,128]{2,1,0:T(8,128)S(1)} %get-tuple-element.32.p0_ref, f32[16,16,128]{2,1,0:T(8,128)S(1)} %get-tuple-element.38.p1_ref, f32[16,216,128]{2,1,0:T(8,128)S(1)} %all-to-all-done.1.fields_ref, f32[384,128]{1,0:T(8,128)S(1)} %collective-permute-done.10.upper_ref, ...), custom_call_target="tpu_custom_call" | custom-call | bytes 11070000 | tf_op jit(solution)/shard_map/pallas_call | solution.py:30
  81.6 1.1 %collective-permute-done.12.refs_1_ = f32[16,128]{1,0:T(8,128)S(1)} collective-permute-done((f32[16,128]{1,0:T(8,128)S(1)}, f32[16,128]{1,0:T(8,128)S(1)}, u32[]{:S(2)}, u32[]{:S(2)}) %collective-permute-start.12) | collective-permute-done | bytes 8224 | tf_op jit(solution)/shard_map/ppermute | solution.py:435
  82.7 1.2 %shard_map.88 = f32[16,4,16,128]{3,2,1,0:T(8,128)S(1)} custom-call(f32[32,16,128]{2,1,0:T(8,128)S(1)} %get-tuple-element.42.a_ref, f32[32,16,128]{2,1,0:T(8,128)S(1)} %get-tuple-element.43.b_ref, f32[32,16,128]{2,1,0:T(8,128)S(1)} %get-tuple-element.44.e_ref, f32[32,16,128]{2,1,0:T(8,128)S(1)} %get-tuple-element.45.f_ref, ...), custom_call_target="tpu_custom_call" | custom-call | bytes 3690000 | tf_op jit(solution)/shard_map/pallas_call | solution.py:30
  83.9 23.1 %all_to_all.15.in_ref = f32[16,4,16,128]{3,2,1,0:T(8,128)S(1)} all-to-all(f32[16,4,16,128]{3,2,1,0:T(8,128)S(1)} %shard_map.88), channel_id=1, replica_groups=mesh['build'=16,'lat'=16] {'build'}, dimensions={0} | all-to-all | bytes 1048576 | tf_op jit(solution)/shard_map/all_to_all | solution.py:439
  107.0 1.0 shard_map.89
  (45 shorter events, 3.0 us)
Async XLA Ops:
  0.6 10.4 %copy-start.2 = (f32[3,2,16,1024]{3,2,1,0:T(8,128)S(1)}, f32[3,2,16,1024]{3,2,1,0:T(8,128)}, u32[]{:S(2)}) copy-start(f32[3,2,16,1024]{3,2,1,0:T(8,128)} %adj_ref.3) | copy-start | bytes 1179652
  0.6 10.4 %copy-start.1 = (f32[3,2,16,1024]{3,2,1,0:T(8,128)S(1)}, f32[3,2,16,1024]{3,2,1,0:T(8,128)}, u32[]{:S(2)}) copy-start(f32[3,2,16,1024]{3,2,1,0:T(8,128)} %disp_ref.3) | copy-start | bytes 1179652
  0.7 1.0 copy-start.3
  1.6 18.3 %copy-start.12 = (s32[16,1024]{1,0:T(8,128)S(1)}, s32[16,1024]{1,0:T(8,128)}, u32[]{:S(2)}) copy-start(s32[16,1024]{1,0:T(8,128)} %mask_ref.1) | copy-start | bytes 196612
  2.6 20.8 %all-to-all-start = ((f32[16,2,16,256]{3,2,1,0:T(8,128)}), f32[16,2,16,256]{3,2,1,0:T(8,128)S(1)}, u32[]{:S(2)}, u32[]{:S(2)}) async-start(f32[16,2,16,256]{3,2,1,0:T(8,128)} %shard_map.77), calls=%async_computation | async-start | bytes 1048576 | tf_op jit(solution)/shard_map/all_to_all | solution.py:439
  11.1 8.9 %collective-permute-start = (f32[16,1024]{1,0:T(8,128)S(1)}, f32[16,1024]{1,0:T(8,128)S(1)}, u32[]{:S(2)}, u32[]{:S(2)}) collective-permute-start(f32[16,1024]{1,0:T(8,128)S(1)} %get-tuple-element.27), channel_id=1, source_target_pairs={{0,1},{1,2},{2,3},{3,4},{4,5},{5,6},{6,7},{7,8},{8,9},{9,10},{10,1... | collective-permute-start | bytes 196616 | tf_op jit(solution)/shard_map/ppermute | solution.py:435
  12.8 7.2 %collective-permute-start.1 = (f32[16,1024]{1,0:T(8,128)S(1)}, f32[16,1024]{1,0:T(8,128)S(1)}, u32[]{:S(2)}, u32[]{:S(2)}) collective-permute-start(f32[16,1024]{1,0:T(8,128)S(1)} %get-tuple-element.28), channel_id=1, source_target_pairs={{1,0},{2,1},{3,2},{4,3},{5,4},{6,5},{7,6},{8,7},{9,8},{10,9},{11,1... | collective-permute-start | bytes 196616 | tf_op jit(solution)/shard_map/ppermute | solution.py:435
  21.0 1.2 %copy-start = (f32[16,216,128]{2,1,0:T(8,128)}, f32[16,216,128]{2,1,0:T(8,128)S(1)}, u32[]{:S(2)}) copy-start(f32[16,216,128]{2,1,0:T(8,128)S(1)} %get-tuple-element.41) | copy-start | bytes 5308420
  23.4 24.2 %copy-start.14 = (f32[8,3,3]{0,2,1:T(4,128)S(1)}, f32[8,3,3]{0,2,1:T(4,128)}, u32[]{:S(2)}) copy-start(f32[8,3,3]{0,2,1:T(4,128)} %param.9) | copy-start | bytes 868
  23.4 38.4 %all-to-all-start.1 = ((f32[16,216,128]{2,1,0:T(8,128)}), f32[16,216,128]{2,1,0:T(8,128)S(1)}, u32[]{:S(2)}, u32[]{:S(2)}) async-start(f32[16,216,128]{2,1,0:T(8,128)} %copy-done), calls=%async_computation.1 | async-start | bytes 3538944 | tf_op jit(solution)/shard_map/all_to_all | solution.py:439
  31.2 11.6 %collective-permute-start.2 = (f32[192,256]{1,0:T(8,128)S(1)}, f32[192,256]{1,0:T(8,128)S(1)}, u32[]{:S(2)}, u32[]{:S(2)}) collective-permute-start(f32[192,256]{1,0:T(8,128)S(1)} %get-tuple-element.30), channel_id=1, source_target_pairs={{0,1},{1,2},{2,3},{3,4},{4,5},{5,6},{6,7},{7,8},{8,9},{9,10},{10,1... | collective-permute-start | bytes 589832 | tf_op jit(solution)/shard_map/ppermute | solution.py:435
  31.2 11.6 %collective-permute-start.3 = (f32[192,256]{1,0:T(8,128)S(1)}, f32[192,256]{1,0:T(8,128)S(1)}, u32[]{:S(2)}, u32[]{:S(2)}) collective-permute-start(f32[192,256]{1,0:T(8,128)S(1)} %get-tuple-element.31), channel_id=1, source_target_pairs={{1,0},{2,1},{3,2},{4,3},{5,4},{6,5},{7,6},{8,7},{9,8},{10,9},{11,1... | collective-permute-start | bytes 589832 | tf_op jit(solution)/shard_map/ppermute | solution.py:435
  34.9 17.6 %collective-permute-start.4 = (f32[176,256]{1,0:T(8,128)}, f32[176,256]{1,0:T(8,128)S(1)}, u32[]{:S(2)}, u32[]{:S(2)}) collective-permute-start(f32[176,256]{1,0:T(8,128)} %get-tuple-element.35), channel_id=1, source_target_pairs={{0,1},{1,2},{2,3},{3,4},{4,5},{5,6},{6,7},{7,8},{8,9},{9,10},{10,1... | collective-permute-start | bytes 540680 | tf_op jit(solution)/shard_map/ppermute | solution.py:435
  34.9 17.6 %collective-permute-start.5 = (f32[176,256]{1,0:T(8,128)}, f32[176,256]{1,0:T(8,128)S(1)}, u32[]{:S(2)}, u32[]{:S(2)}) collective-permute-start(f32[176,256]{1,0:T(8,128)} %get-tuple-element.36), channel_id=1, source_target_pairs={{1,0},{2,1},{3,2},{4,3},{5,4},{6,5},{7,6},{8,7},{9,8},{10,9},{11,1... | collective-permute-start | bytes 540680 | tf_op jit(solution)/shard_map/ppermute | solution.py:435
  44.8 0.6 copy-start.6
  45.4 7.1 %copy-start.4 = (f32[16,16,128]{2,1,0:T(8,128)}, f32[16,16,128]{2,1,0:T(8,128)S(1)}, u32[]{:S(2)}) copy-start(f32[16,16,128]{2,1,0:T(8,128)S(1)} %get-tuple-element.33.g0_ref) | copy-start | bytes 393220
  45.4 7.0 %collective-permute-start.7 = (f32[16,256]{1,0:T(8,128)S(1)}, f32[16,256]{1,0:T(8,128)S(1)}, u32[]{:S(2)}, u32[]{:S(2)}) collective-permute-start(f32[16,256]{1,0:T(8,128)S(1)} %get-tuple-element.37.own_ref), channel_id=1, source_target_pairs={{1,0},{2,1},{3,2},{4,3},{5,4},{6,5},{7,6},{8,7},{9,8},{10,9},{11,1... | collective-permute-start | bytes 49160 | tf_op jit(solution)/shard_map/ppermute | solution.py:435
  47.5 6.1 %collective-permute-start.6 = (f32[16,256]{1,0:T(8,128)S(1)}, f32[16,256]{1,0:T(8,128)}, u32[]{:S(2)}, u32[]{:S(2)}) collective-permute-start(f32[16,256]{1,0:T(8,128)S(1)} %get-tuple-element.37.own_ref), channel_id=1, source_target_pairs={{0,1},{1,2},{2,3},{3,4},{4,5},{5,6},{6,7},{7,8},{8,9},{9,10},{10,1... | collective-permute-start | bytes 49160 | tf_op jit(solution)/shard_map/ppermute | solution.py:435
  47.6 0.7 copy-start.13
  56.9 0.7 copy-start.8
  57.5 0.6 copy-start.10
  58.2 6.6 %copy-start.5 = (f32[16,16,128]{2,1,0:T(8,128)S(1)}, f32[16,16,128]{2,1,0:T(8,128)}, u32[]{:S(2)}) copy-start(f32[16,16,128]{2,1,0:T(8,128)} %copy-done.4) | copy-start | bytes 393220
  61.8 2.9 %copy-start.9 = (f32[16,16,128]{2,1,0:T(8,128)S(1)}, f32[16,16,128]{2,1,0:T(8,128)}, u32[]{:S(2)}) copy-start(f32[16,16,128]{2,1,0:T(8,128)} %copy-done.8) | copy-start | bytes 393220
  61.8 2.9 %copy-start.11 = (f32[16,16,128]{2,1,0:T(8,128)S(1)}, f32[16,16,128]{2,1,0:T(8,128)}, u32[]{:S(2)}) copy-start(f32[16,16,128]{2,1,0:T(8,128)} %copy-done.10) | copy-start | bytes 393220
  64.8 0.9 copy-start.7
  65.8 7.6 %collective-permute-start.10 = (f32[384,128]{1,0:T(8,128)S(1)}, f32[384,128]{1,0:T(8,128)S(1)}, u32[]{:S(2)}, u32[]{:S(2)}) collective-permute-start(f32[384,128]{1,0:T(8,128)S(1)} %get-tuple-element.48), channel_id=1, source_target_pairs={{0,1},{1,2},{2,3},{3,4},{4,5},{5,6},{6,7},{7,8},{8,9},{9,10},{10,1... | collective-permute-start | bytes 589832 | tf_op jit(solution)/shard_map/ppermute | solution.py:435
  65.9 7.5 %collective-permute-start.11 = (f32[384,128]{1,0:T(8,128)S(1)}, f32[384,128]{1,0:T(8,128)S(1)}, u32[]{:S(2)}, u32[]{:S(2)}) collective-permute-start(f32[384,128]{1,0:T(8,128)S(1)} %get-tuple-element.49), channel_id=1, source_target_pairs={{1,0},{2,1},{3,2},{4,3},{5,4},{6,5},{7,6},{8,7},{9,8},{10,9},{11,1... | collective-permute-start | bytes 589832 | tf_op jit(solution)/shard_map/ppermute | solution.py:435
  69.9 11.7 %collective-permute-start.8 = (f32[352,128]{1,0:T(8,128)S(1)}, f32[352,128]{1,0:T(8,128)S(1)}, u32[]{:S(2)}, u32[]{:S(2)}) collective-permute-start(f32[352,128]{1,0:T(8,128)S(1)} %get-tuple-element.46), channel_id=1, source_target_pairs={{0,1},{1,2},{2,3},{3,4},{4,5},{5,6},{6,7},{7,8},{8,9},{9,10},{10,1... | collective-permute-start | bytes 540680 | tf_op jit(solution)/shard_map/ppermute | solution.py:435
  69.9 11.7 %collective-permute-start.9 = (f32[352,128]{1,0:T(8,128)S(1)}, f32[352,128]{1,0:T(8,128)S(1)}, u32[]{:S(2)}, u32[]{:S(2)}) collective-permute-start(f32[352,128]{1,0:T(8,128)S(1)} %get-tuple-element.47), channel_id=1, source_target_pairs={{1,0},{2,1},{3,2},{4,3},{5,4},{6,5},{7,6},{8,7},{9,8},{10,9},{11,1... | collective-permute-start | bytes 540680 | tf_op jit(solution)/shard_map/ppermute | solution.py:435
  74.6 7.0 %collective-permute-start.13 = (f32[16,128]{1,0:T(8,128)S(1)}, f32[16,128]{1,0:T(8,128)S(1)}, u32[]{:S(2)}, u32[]{:S(2)}) collective-permute-start(f32[16,128]{1,0:T(8,128)S(1)} %get-tuple-element.50.refs_0_), channel_id=1, source_target_pairs={{1,0},{2,1},{3,2},{4,3},{5,4},{6,5},{7,6},{8,7},{9,8},{10,9},{11,1... | collective-permute-start | bytes 24584 | tf_op jit(solution)/shard_map/ppermute | solution.py:435
  78.0 4.6 %collective-permute-start.12 = (f32[16,128]{1,0:T(8,128)S(1)}, f32[16,128]{1,0:T(8,128)S(1)}, u32[]{:S(2)}, u32[]{:S(2)}) collective-permute-start(f32[16,128]{1,0:T(8,128)S(1)} %get-tuple-element.50.refs_0_), channel_id=1, source_target_pairs={{0,1},{1,2},{2,3},{3,4},{4,5},{5,6},{6,7},{7,8},{8,9},{9,10},{10,1... | collective-permute-start | bytes 24584 | tf_op jit(solution)/shard_map/ppermute | solution.py:435
